TPU v7x, 32 devices: a whole 2x2x4 slice. The times are simulated.
32 devices in a mesh: dp: 8 (over z, x), tensor: 4 (over y, core).
Axes of the slice: x: 2, y: 2, z: 4, core: 2. Of those that a mesh axis runs over, the one named last changes fastest.
Arguments:
- tokens: bfloat16 [2, 1024, 8, 768], P(None, 'tensor', 'dp'), may hold values from -6 to 6
- segment_ids: int32 [2, 8, 1024], P(None, 'dp'), may hold values from 0 to 17, as said below
- valid_mask: int32 [2, 8, 1024], P(None, 'dp'), may hold values from 0 to 1, as said below
- gain_one: float32 [768], replicated, may hold values from 0.5 to 1.5
- shift_one: float32 [768], replicated, may hold values from -1.25 to 1.25
- w_qkv: bfloat16 [768, 3, 768], P(None, None, 'tensor'), may hold values from -0.21875 to 0.21875
- bias_qv: float32 [2, 768], P(None, 'tensor'), may hold values from -1.75 to 1.75
- output_weight: bfloat16 [768, 768], P('tensor'), may hold values from -1.75 to 1.75
- bias_out: float32 [768], replicated, may hold values from -1.25 to 1.25
- gain_two: float32 [768], replicated, may hold values from 0.5 to 1.5
- shift_two: float32 [768], replicated, may hold values from -1.25 to 1.25
- up_weight: bfloat16 [768, 3072], P(None, 'tensor'), may hold values from -0.21875 to 0.21875
- bias_up: float32 [3072], P('tensor'), may hold values from -1.75 to 1.75
- down_weight: bfloat16 [3072, 768], P('tensor'), may hold values from -0.109375 to 0.109375
- bias_down: float32 [768], replicated, may hold values from -1.25 to 1.25
- out_grad: bfloat16 [2, 1024, 8, 768], P(None, 'tensor', 'dp'), may hold values from -6 to 6
Outputs:
- block_out: bfloat16 [2, 1024, 8, 768], P(None, 'tensor', 'dp')
- grad_tokens: float32 [2, 1024, 8, 768], P(None, 'tensor', 'dp')
- grad_gain_one: float32 [768], replicated
- grad_shift_one: float32 [768], replicated
- grad_w_qkv: float32 [768, 3, 768], P('dp', None, 'tensor')
- grad_bias_qv: float32 [2, 768], P(None, 'tensor')
- grad_w_out: float32 [768, 768], P('tensor', 'dp')
- grad_bias_out: float32 [768], replicated
- grad_gain_two: float32 [768], replicated
- grad_shift_two: float32 [768], replicated
- grad_w_up: float32 [768, 3072], P('dp', 'tensor')
- grad_bias_up: float32 [3072], P('tensor')
- grad_w_down: float32 [3072, 768], P('tensor', 'dp')
- grad_bias_down: float32 [768], replicated
Inputs may be any that keep to these rules, and one draw needn't show every extreme that they name: `segment_ids`: within a sequence ids never fall; its documents hold 60 to 800 tokens, except the last, which the sequence's end cuts. `valid_mask`: each sequence has ones on a leading run of at least 768 positions and zeros after it.
All inputs are finite; a program needn't handle non-finite values.
Results may differ from a plain program's by a relative error of at most 0.012.
The roundings to bfloat16 on the way count: a program that leaves them out, or rounds other values in their place, can miss the bound.
Values may be sent and summed in bfloat16 or wider, within the bound.
A program may use at most 128 MiB of HBM per device.

v0:
```python
import jax
import jax.numpy as jnp
from jax import lax
from jax.sharding import PartitionSpec as P

HEAD_DIM = 64


eps_norm = 1e-06
masked_score = -1e30


def gelu_tanh(values):
    return jax.nn.gelu(values, approximate=True)


def norm_forward(rows, gain, shift):
    mean = jnp.mean(rows, axis=-1, keepdims=True)
    centred = rows - mean
    factor = lax.rsqrt(jnp.mean(centred * centred, axis=-1, keepdims=True) + eps_norm)
    normal = centred * factor
    return (normal * gain + shift, normal, factor)


def norm_backward(grad, normal, factor, gain):
    inner = grad * gain
    first = jnp.mean(inner, axis=-1, keepdims=True)
    second = jnp.mean(inner * normal, axis=-1, keepdims=True)
    return factor * (inner - first - normal * second)


def block_scores(queries, keys_all, seg, valid, start, size):
    rows_q = lax.dynamic_slice_in_dim(queries, start, size)
    factor = queries.shape[-1] ** (-0.5)
    scores = (
        jnp.einsum("qhd,khd->hqk", rows_q, keys_all, preferred_element_type=jnp.float32) * factor
    )
    seg_rows = lax.dynamic_slice_in_dim(seg, start, size)
    place_rows = start + jnp.arange(size, dtype=jnp.int32)
    place_cols = jnp.arange(seg.shape[0], dtype=jnp.int32)
    same = (seg_rows[:, None] == seg[None, :]) & (valid[None, :] > 0)
    allowed = same | (place_rows[:, None] == place_cols[None, :])
    return (jnp.where(allowed[None], scores, masked_score), rows_q)


def attend(item):
    queries, keys_all, values_all, seg, valid = item
    length = queries.shape[0]
    size = min(512, length)

    def block_step(start):
        scores, rows_q = block_scores(queries, keys_all, seg, valid, start, size)
        top = jnp.max(scores, axis=-1, keepdims=True)
        total = jnp.sum(jnp.exp(scores - top), axis=-1, keepdims=True)
        log_total = top + jnp.log(total)
        probs = jnp.exp(scores - log_total).astype(jnp.bfloat16)
        mixed = jnp.einsum("hqk,khd->qhd", probs, values_all, preferred_element_type=jnp.float32)
        return (mixed, log_total[..., 0])

    starts = jnp.arange(length // size, dtype=jnp.int32) * size
    mixed, log_total = lax.map(block_step, starts)
    return (mixed.reshape(length, -1), log_total)


def attend_back(item):
    queries, keys_all, values_all, seg, valid, log_total, grad_mixed = item
    length = queries.shape[0]
    size = min(512, length)
    factor = queries.shape[-1] ** (-0.5)

    def block_step(carry, piece):
        start, log_block = piece
        key_grad, value_grad = carry
        scores, rows_q = block_scores(queries, keys_all, seg, valid, start, size)
        probs = jnp.exp(scores - log_block[..., None])
        probs_low = probs.astype(jnp.bfloat16)
        grad_rows = lax.dynamic_slice_in_dim(grad_mixed, start, size)
        value_grad = value_grad + jnp.einsum(
            "hqk,qhd->khd", probs_low, grad_rows, preferred_element_type=jnp.float32
        )
        grad_probs = jnp.einsum(
            "qhd,khd->hqk", grad_rows, values_all, preferred_element_type=jnp.float32
        )
        inner = jnp.sum(probs * grad_probs, axis=-1, keepdims=True)
        grad_scores = (probs * (grad_probs - inner)).astype(jnp.bfloat16)
        query_grad = (
            jnp.einsum("hqk,khd->qhd", grad_scores, keys_all, preferred_element_type=jnp.float32)
            * factor
        )
        key_grad = (
            key_grad
            + jnp.einsum("hqk,qhd->khd", grad_scores, rows_q, preferred_element_type=jnp.float32)
            * factor
        )
        return ((key_grad, value_grad), query_grad)

    starts = jnp.arange(length // size, dtype=jnp.int32) * size
    zeros = jnp.zeros(keys_all.shape, jnp.float32)
    (key_grad, value_grad), query_grad = lax.scan(block_step, (zeros, zeros), (starts, log_total))
    return (query_grad.reshape(keys_all.shape), key_grad, value_grad)


def body(
    tokens,
    segment_ids,
    valid_mask,
    gain_one,
    shift_one,
    w_qkv,
    bias_qv,
    output_weight,
    bias_out,
    gain_two,
    shift_two,
    up_weight,
    bias_up,
    down_weight,
    bias_down,
    out_grad,
):
    micro, rows, seqs, width = tokens.shape
    local = w_qkv.shape[2]
    heads = local // HEAD_DIM
    w_joined = w_qkv.reshape(width, 3 * local)
    results = []
    input_grads = []
    totals = None
    small = (jnp.zeros((width,), jnp.float32),) * 6
    bias_qv_grad = jnp.zeros(bias_qv.shape, jnp.float32)
    bias_up_grad = jnp.zeros(bias_up.shape, jnp.float32)
    for step in range(micro):
        start_rows = tokens[step].astype(jnp.float32)
        normed, normal_one, factor_one = norm_forward(start_rows, gain_one, shift_one)
        normed_all = lax.all_gather(normed.astype(jnp.bfloat16), "tensor", axis=0, tiled=True)
        length = normed_all.shape[0]
        joined = jnp.einsum("lsd,de->lse", normed_all, w_joined, preferred_element_type=jnp.float32)
        queries = (joined[..., :local] + bias_qv[0]).astype(jnp.bfloat16)
        keys_all = joined[..., local : 2 * local].astype(jnp.bfloat16)
        values_all = (joined[..., 2 * local :] + bias_qv[1]).astype(jnp.bfloat16)

        def split(values):
            return jnp.moveaxis(values, 1, 0).reshape(seqs, length, heads, HEAD_DIM)

        def merge_back(values):
            return jnp.moveaxis(values.reshape(seqs, length, local), 0, 1)

        seg_now = segment_ids[step]
        valid_now = valid_mask[step]
        head_q, head_k, head_v = (split(queries), split(keys_all), split(values_all))
        mixed, log_total = lax.map(attend, (head_q, head_k, head_v, seg_now, valid_now))
        mixed_reduced_precision = jnp.moveaxis(mixed, 0, 1).astype(jnp.bfloat16)
        attn = (
            lax.psum_scatter(
                jnp.einsum(
                    "grn,nd->grd",
                    mixed_reduced_precision,
                    output_weight,
                    preferred_element_type=jnp.float32,
                ),
                "tensor",
                scatter_dimension=0,
                tiled=True,
            )
            + bias_out
        )
        middle = start_rows + attn
        normed_two, normal_two, factor_two = norm_forward(middle, gain_two, shift_two)
        second_normed_gathered = lax.all_gather(
            normed_two.astype(jnp.bfloat16), "tensor", axis=0, tiled=True
        )
        upper = (
            jnp.einsum(
                "nhe,em->nhm", second_normed_gathered, up_weight, preferred_element_type=jnp.float32
            )
            + bias_up
        )
        hidden, gelu_pull = jax.vjp(gelu_tanh, upper)
        hidden_reduced_precision = hidden.astype(jnp.bfloat16)
        branch = (
            lax.psum_scatter(
                jnp.einsum(
                    "pxm,mk->pxk",
                    hidden_reduced_precision,
                    down_weight,
                    preferred_element_type=jnp.float32,
                ).astype(jnp.bfloat16),
                "tensor",
                scatter_dimension=0,
                tiled=True,
            ).astype(jnp.float32)
            + bias_down
        )
        results.append((middle + branch).astype(jnp.bfloat16))
        grad_rows = out_grad[step]
        gathered_gradient = lax.all_gather(grad_rows, "tensor", axis=0, tiled=True)
        step_down = jnp.einsum(
            "xrm,xrc->mc",
            hidden_reduced_precision,
            gathered_gradient,
            preferred_element_type=jnp.float32,
        )
        grad_hidden = jnp.einsum(
            "hci,gi->hcg", gathered_gradient, down_weight, preferred_element_type=jnp.float32
        )
        upper_branch_gradient = gelu_pull(grad_hidden)[0].astype(jnp.bfloat16)
        step_up = jnp.einsum(
            "yap,yab->pb",
            second_normed_gathered,
            upper_branch_gradient,
            preferred_element_type=jnp.float32,
        )
        bias_up_grad = bias_up_grad + jnp.sum(
            upper_branch_gradient.astype(jnp.float32), axis=(0, 1)
        )
        grad_normed_two = lax.psum_scatter(
            jnp.einsum(
                "pav,zv->paz", upper_branch_gradient, up_weight, preferred_element_type=jnp.float32
            ),
            "tensor",
            scatter_dimension=0,
            tiled=True,
        )
        grad_middle = grad_rows.astype(jnp.float32) + norm_backward(
            grad_normed_two, normal_two, factor_two, gain_two
        )
        grad_attn = grad_middle.astype(jnp.bfloat16)
        grad_attn_all = lax.all_gather(grad_attn, "tensor", axis=0, tiled=True)
        step_out = jnp.einsum(
            "lse,lsd->ed",
            mixed_reduced_precision,
            grad_attn_all,
            preferred_element_type=jnp.float32,
        )
        grad_mixed = jnp.einsum(
            "lsd,ed->lse", grad_attn_all, output_weight, preferred_element_type=jnp.float32
        ).astype(jnp.bfloat16)
        query_grad, key_grad, value_grad = lax.map(
            attend_back, (head_q, head_k, head_v, seg_now, valid_now, log_total, split(grad_mixed))
        )
        query_low = merge_back(query_grad).astype(jnp.bfloat16)
        key_low = merge_back(key_grad).astype(jnp.bfloat16)
        value_low = merge_back(value_grad).astype(jnp.bfloat16)
        bias_qv_grad = bias_qv_grad + jnp.stack(
            [
                jnp.sum(query_low.astype(jnp.float32), axis=(0, 1)),
                jnp.sum(value_low.astype(jnp.float32), axis=(0, 1)),
            ]
        )
        grad_joined_rows = jnp.concatenate([query_low, key_low, value_low], axis=-1)
        step_joined = jnp.einsum(
            "lsd,lse->de", normed_all, grad_joined_rows, preferred_element_type=jnp.float32
        )
        grad_normed = lax.psum_scatter(
            jnp.einsum(
                "lse,de->lsd", grad_joined_rows, w_joined, preferred_element_type=jnp.float32
            ),
            "tensor",
            scatter_dimension=0,
            tiled=True,
        )
        input_grads.append(
            grad_middle + norm_backward(grad_normed, normal_one, factor_one, gain_one)
        )
        small = (
            small[0] + jnp.sum(grad_normed * normal_one, axis=(0, 1)),
            small[1] + jnp.sum(grad_normed, axis=(0, 1)),
            small[2] + jnp.sum(grad_attn.astype(jnp.float32), axis=(0, 1)),
            small[3] + jnp.sum(grad_normed_two * normal_two, axis=(0, 1)),
            small[4] + jnp.sum(grad_normed_two, axis=(0, 1)),
            small[5] + jnp.sum(grad_rows.astype(jnp.float32), axis=(0, 1)),
        )
        terms = (step_joined, step_out, step_up, step_down)
        totals = terms if totals is None else jax.tree.map(jnp.add, totals, terms)
    shares = (
        lax.psum_scatter(totals[0], "dp", scatter_dimension=0, tiled=True),
        lax.psum_scatter(totals[1], "dp", scatter_dimension=1, tiled=True),
        lax.psum_scatter(totals[2], "dp", scatter_dimension=0, tiled=True),
        lax.psum_scatter(totals[3], "dp", scatter_dimension=1, tiled=True),
    )
    bias_shares = lax.psum((bias_qv_grad, bias_up_grad), "dp")
    norm_shares = lax.psum(
        (small[0], small[1], small[2], small[3], small[4], small[5]), ("dp", "tensor")
    )
    grad_qkv = shares[0].reshape(shares[0].shape[0], 3, local)
    return (
        jnp.stack(results),
        jnp.stack(input_grads),
        norm_shares[0],
        norm_shares[1],
        grad_qkv,
        bias_shares[0],
        shares[1],
        norm_shares[2],
        norm_shares[3],
        norm_shares[4],
        shares[2],
        bias_shares[1],
        shares[3],
        norm_shares[5],
    )


def solution(mesh):
    placed = (
        P(None, "tensor", "dp", None),
        P(None, "dp", None),
        P(None, "dp", None),
        P(),
        P(),
        P(None, None, "tensor"),
        P(None, "tensor"),
        P("tensor", None),
        P(),
        P(),
        P(),
        P(None, "tensor"),
        P("tensor"),
        P("tensor", None),
        P(),
        P(None, "tensor", "dp", None),
    )
    return jax.shard_map(
        body,
        mesh=mesh,
        in_specs=placed,
        out_specs=(
            P(None, "tensor", "dp", None),
            P(None, "tensor", "dp", None),
            P(),
            P(),
            P("dp", None, "tensor"),
            P(None, "tensor"),
            P("tensor", "dp"),
            P(),
            P(),
            P(),
            P("dp", "tensor"),
            P("tensor"),
            P("tensor", "dp"),
            P(),
        ),
        check_vma=False,
    )
```

profile of v0, /device:TPU:0, one launch (start us, length us, event | category | flops | bytes accessed | tf_op | source)
XLA Modules:
  0.0 860.0 jit_solution(4790978515740681391)
XLA Ops:
  14.1 21.1 %all-gather.15.cloned.1.call-done = bf16[1024,1,768]{2,0,1:T(8,128)(2,1)} async-done(((bf16[256,1,768]{2,0,1:T(8,128)(2,1)}), bf16[1024,1,768]{2,0,1:T(8,128)(2,1)}) %all-gather.15.cloned.1.call-update) | async-done | bytes 1572880 | tf_op jit(solution)/shard_map/all_gather | solution.py:134
  39.2 17.8 %all-gather.11.cloned.1.call-done = bf16[1024,1,768]{2,0,1:T(8,128)(2,1)} async-done(((bf16[256,1,768]{2,0,1:T(8,128)(2,1)}), bf16[1024,1,768]{2,0,1:T(8,128)(2,1)}) %all-gather.11.cloned.1.call-update) | async-done | bytes 1572880 | tf_op jit(solution)/shard_map/all_gather | solution.py:134
  62.2 20.0 %while.95 = (s32[]{:T(128)}, bf16[2,512,3,64]{1,3,2,0:T(8,128)(2,1)S(1)}, f32[2,3,512]{2,1,0:T(4,128)}, s32[2]{0:T(128)}, s32[1024]{0:T(1024)S(1)}, /*index=5*/s...) while((s32[]{:T(128)}, ...), condition=%wide.region_15.16_spmd, body=%wide.region_12.15_spmd.sunk | while | flops 422051840 | bytes 22526200 | solution.py:61
  88.9 20.0 %while.94 = (s32[]{:T(128)}, bf16[2,512,3,64]{1,3,2,0:T(8,128)(2,1)S(1)}, f32[2,3,512]{2,1,0:T(4,128)}, s32[2]{0:T(128)}, s32[1024]{0:T(1024)S(1)}, /*index=5*/s...) while((s32[]{:T(128)}, ...), condition=%wide.region_5.6_spmd, body=%wide.region_2.5_spmd.sunk | while | flops 422051840 | bytes 22526200 | solution.py:61
  113.8 10.9 %reduce-scatter.19.cloned.1.call-done = f32[256,1,768]{2,0,1:T(8,128)} async-done(((f32[1024,1,768]{2,0,1:T(8,128)}), f32[256,1,768]{2,0,1:T(8,128)}) %reduce-scatter.19.cloned.1.call-update) | async-done | bytes 786448 | tf_op jit(solution)/shard_map/reduce_scatter | solution.py:153
  124.7 40.3 %reduce-scatter.15.cloned.1.call-done = f32[256,1,768]{2,0,1:T(8,128)} async-done(((f32[1024,1,768]{2,0,1:T(8,128)}), f32[256,1,768]{2,0,1:T(8,128)}) %reduce-scatter.15.cloned.1.call-update) | async-done | bytes 786448 | tf_op jit(solution)/shard_map/reduce_scatter | solution.py:153
  171.5 17.2 %all-gather.17.cloned.1.call-done = bf16[1024,1,768]{2,0,1:T(8,128)(2,1)} async-done(((bf16[256,1,768]{2,0,1:T(8,128)(2,1)}), bf16[1024,1,768]{2,0,1:T(8,128)(2,1)}) %all-gather.17.cloned.1.call-update) | async-done | bytes 1572880 | tf_op jit(solution)/shard_map/all_gather | solution.py:168
  188.7 4.8 fusion.112
  193.5 16.3 %all-gather.25.cloned.1.call-done = bf16[1,1024,1,768]{3,1,2,0:T(8,128)(2,1)} async-done(((bf16[1,256,1,768]{3,1,2,0:T(8,128)(2,1)}), bf16[1,1024,1,768]{3,1,2,0:T(8,128)(2,1)}) %all-gather.25.cloned.1.call-update) | async-done | bytes 1572880 | tf_op jit(solution)/shard_map/all_gather | solution.py:195
  209.8 6.3 convert_reduce_fusion
  221.0 10.6 %all-gather.13.cloned.1.call-done = bf16[1024,1,768]{2,0,1:T(8,128)(2,1)} async-done(((bf16[256,1,768]{2,0,1:T(8,128)(2,1)}), bf16[1024,1,768]{2,0,1:T(8,128)(2,1)}) %all-gather.13.cloned.1.call-update) | async-done | bytes 1572880 | tf_op jit(solution)/shard_map/all_gather | solution.py:168
  231.6 4.8 fusion.119
  236.4 16.4 %all-gather.23.cloned.1.call-done = bf16[1,1024,1,768]{3,1,2,0:T(8,128)(2,1)} async-done(((bf16[1,256,1,768]{3,1,2,0:T(8,128)(2,1)}), bf16[1,1024,1,768]{3,1,2,0:T(8,128)(2,1)}) %all-gather.23.cloned.1.call-update) | async-done | bytes 1572880 | tf_op jit(solution)/shard_map/all_gather | solution.py:195
  252.8 6.3 convert_reduce_fusion.1
  263.5 5.4 fusion.131
  269.0 5.3 fusion.130
  274.3 18.9 %reduce-scatter.27.cloned.1.call-done = f32[256,1,768]{2,0,1:T(8,128)} async-done(((f32[1024,1,768]{2,0,1:T(8,128)}), f32[256,1,768]{2,0,1:T(8,128)}) %reduce-scatter.27.cloned.1.call-update) | async-done | bytes 786448 | tf_op jit(solution)/shard_map/reduce_scatter | solution.py:215
  293.3 40.3 %reduce-scatter.23.cloned.1.call-done = f32[256,1,768]{2,0,1:T(8,128)} async-done(((f32[1024,1,768]{2,0,1:T(8,128)}), f32[256,1,768]{2,0,1:T(8,128)}) %reduce-scatter.23.cloned.1.call-update) | async-done | bytes 786448 | tf_op jit(solution)/shard_map/reduce_scatter | solution.py:215
  336.6 28.1 %reduce-scatter.21.cloned.1.call-done = bf16[256,1,768]{2,0,1:T(8,128)(2,1)} async-done(((bf16[1024,1,768]{2,0,1:T(8,128)(2,1)}), bf16[256,1,768]{2,0,1:T(8,128)(2,1)}) %reduce-scatter.21.cloned.1.call-update) | async-done | bytes 393232 | tf_op jit(solution)/shard_map/reduce_scatter | solution.py:180
  364.7 30.4 %reduce-scatter.17.cloned.1.call-done = bf16[256,1,768]{2,0,1:T(8,128)(2,1)} async-done(((bf16[1024,1,768]{2,0,1:T(8,128)(2,1)}), bf16[256,1,768]{2,0,1:T(8,128)(2,1)}) %reduce-scatter.17.cloned.1.call-update) | async-done | bytes 393232 | tf_op jit(solution)/shard_map/reduce_scatter | solution.py:180
  395.2 4.9 convert_reduce_fusion.7
  400.9 19.0 %all-gather.21.cloned.1.call-done = bf16[1024,1,768]{2,0,1:T(8,128)(2,1)} async-done(((bf16[256,1,768]{2,0,1:T(8,128)(2,1)}), bf16[1024,1,768]{2,0,1:T(8,128)(2,1)}) %all-gather.21.cloned.1.call-update) | async-done | bytes 1572880 | tf_op jit(solution)/shard_map/all_gather | solution.py:227
  423.5 29.4 %while.97 = (s32[]{:T(128)}, f32[1024,3,64]{0,2,1:T(8,128)S(1)}, f32[1024,3,64]{0,2,1:T(8,128)}, bf16[2,512,3,64]{1,3,2,0:T(8,128)(2,1)}, s32[2]{0:T(128)}, /*in...) while((s32[]{:T(128)}, f32[1024,3,64]{0,2,1:T(8,128)S(1)}, ...), condition=%wide.region_34.35_spmd.clone, body=%wide.region_32.34_spmd.clone.sunk | while | flops 1033404416 | bytes 65866100 | solution.py:99
  455.9 28.5 %while.96 = (s32[]{:T(128)}, f32[1024,3,64]{0,2,1:T(8,128)S(1)}, f32[1024,3,64]{0,2,1:T(8,128)}, bf16[2,512,3,64]{1,3,2,0:T(8,128)(2,1)S(1)}, s32[2]{0:T(128)S(1...) while((s32[]{:T(128)}, f32[1024,3,64]{0,2,1:T(8,128)S(1)}, ...), condition=%wide.region_25.26_spmd.clone, body=%wide.region_23.25_spmd.clone.sunk | while | flops 1033404416 | bytes 61147428 | solution.py:99
  501.0 4.4 convolution_bitcast_fusion.2
  534.9 22.3 %all-reduce.1 = (f32[2,192]{1,0:T(2,128)}, f32[768]{0:T(1024)}) all-reduce(f32[2,192]{1,0:T(2,128)S(1)} %maximum_add_fusion, f32[768]{0:T(1024)} %add.444), channel_id=1, replica_groups=mesh['dp'=8,'tensor'=4] {'dp'}, use_global_device_ids=true, to_apply=%region_49.50 | all-reduce | flops 1152 | bytes 9216 | tf_op jit(solution)/shard_map/psum | solution.py:280
  558.8 67.7 %reduce-scatter.31.cloned.1.call-done = f32[96,576]{1,0:T(8,128)} async-done(((f32[768,576]{1,0:T(8,128)}), f32[96,576]{1,0:T(8,128)}) %reduce-scatter.31.cloned.1.call-update) | async-done | bytes 221200 | tf_op jit(solution)/shard_map/reduce_scatter | solution.py:275
  628.4 37.2 %reduce-scatter.25.cloned.1.call-done = f32[256,1,768]{2,0,1:T(8,128)} async-done(((f32[1024,1,768]{2,0,1:T(8,128)}), f32[256,1,768]{2,0,1:T(8,128)}) %reduce-scatter.25.cloned.1.call-update) | async-done | bytes 786448 | tf_op jit(solution)/shard_map/reduce_scatter | solution.py:253
  665.6 40.3 %reduce-scatter.29.cloned.1.call-done = f32[256,1,768]{2,0,1:T(8,128)} async-done(((f32[1024,1,768]{2,0,1:T(8,128)}), f32[256,1,768]{2,0,1:T(8,128)}) %reduce-scatter.29.cloned.1.call-update) | async-done | bytes 786448 | tf_op jit(solution)/shard_map/reduce_scatter | solution.py:253
  713.1 40.7 %all-reduce = (f32[768]{0:T(1024)}, f32[768]{0:T(1024)}, f32[768]{0:T(1024)}, f32[768]{0:T(1024)}, f32[768]{0:T(1024)}, /*index=5*/f32[768]{0:T(1024)}) all-reduce(f32[768]{0:T(1024)S(1)} %add.435, f32[768]{0:T(1024)S(1)} %add.436, f32[768]{0:T(1024)S(1)} %copy-done.63, ...), channel_id=1, replica_groups=mesh['dp'=8,'tensor'=4] {'dp','tensor'}, use_global_device_ids=true, to_apply=%region_40.41 | all-reduce | flops 4608 | bytes 36864 | tf_op jit(solution)/shard_map/psum | solution.py:281
  753.7 26.4 %reduce-scatter.35.cloned.1.call-done = f32[768,96]{0,1:T(8,128)} async-done(((f32[768,768]{0,1:T(8,128)}), f32[768,96]{0,1:T(8,128)}) %reduce-scatter.35.cloned.1.call-update) | async-done | bytes 294928 | tf_op jit(solution)/shard_map/reduce_scatter | solution.py:278
  780.1 72.8 %reduce-scatter.33.cloned.1.call-done = f32[96,768]{1,0:T(8,128)} async-done(((f32[768,768]{1,0:T(8,128)}), f32[96,768]{1,0:T(8,128)}) %reduce-scatter.33.cloned.1.call-update) | async-done | bytes 294928 | tf_op jit(solution)/shard_map/reduce_scatter | solution.py:277
  (412 shorter events, 191.6 us)
Async XLA Ops:
  7.2 202.6 %copy-start = (bf16[768,768]{1,0:T(8,128)(2,1)S(1)}, bf16[768,768]{1,0:T(8,128)(2,1)}, u32[]{:S(2)}) copy-start(bf16[768,768]{1,0:T(8,128)(2,1)} %param.37) | copy-start | bytes 3538948
  7.2 27.9 %all-gather.15.cloned.1.call-start = ((), (), s32[]{:S(2)}) async-start(), calls=%async_computation.16 | async-start | bytes 1966080 | tf_op jit(solution)/shard_map/all_gather | solution.py:134
  12.7 44.3 %all-gather.11.cloned.1.call-start = ((), (), s32[]{:S(2)}) async-start(), calls=%async_computation.12 | async-start | bytes 1966080 | tf_op jit(solution)/shard_map/all_gather | solution.py:134
  13.4 111.3 %reduce-scatter.19.cloned.1.call-start = ((), (), s32[]{:S(2)}) async-start(), calls=%async_computation.17 | async-start | bytes 3932160 | tf_op jit(solution)/shard_map/reduce_scatter | solution.py:153
  86.7 78.3 %reduce-scatter.15.cloned.1.call-start = ((), (), s32[]{:S(2)}) async-start(), calls=%async_computation.13 | async-start | bytes 3932160 | tf_op jit(solution)/shard_map/reduce_scatter | solution.py:153
  113.8 75.0 %all-gather.17.cloned.1.call-start = ((), (), s32[]{:S(2)}) async-start(), calls=%async_computation.18 | async-start | bytes 1966080 | tf_op jit(solution)/shard_map/all_gather | solution.py:168
  168.9 40.9 %all-gather.25.cloned.1.call-start = ((), (), s32[]{:S(2)}) async-start(), calls=%async_computation.30 | async-start | bytes 1966080 | tf_op jit(solution)/shard_map/all_gather | solution.py:195
  170.0 61.6 %all-gather.13.cloned.1.call-start = ((), (), s32[]{:S(2)}) async-start(), calls=%async_computation.14 | async-start | bytes 1966080 | tf_op jit(solution)/shard_map/all_gather | solution.py:168
  170.7 82.1 %all-gather.23.cloned.1.call-start = ((), (), s32[]{:S(2)}) async-start(), calls=%async_computation.29 | async-start | bytes 1966080 | tf_op jit(solution)/shard_map/all_gather | solution.py:195
  171.5 121.8 %reduce-scatter.27.cloned.1.call-start = ((), (), s32[]{:S(2)}) async-start(), calls=%async_computation.23 | async-start | bytes 3932160 | tf_op jit(solution)/shard_map/reduce_scatter | solution.py:215
  220.4 113.2 %reduce-scatter.23.cloned.1.call-start = ((), (), s32[]{:S(2)}) async-start(), calls=%async_computation.20 | async-start | bytes 3932160 | tf_op jit(solution)/shard_map/reduce_scatter | solution.py:215
  263.4 101.3 %reduce-scatter.21.cloned.1.call-start = ((), (), s32[]{:S(2)}) async-start(), calls=%async_computation.19 | async-start | bytes 1966080 | tf_op jit(solution)/shard_map/reduce_scatter | solution.py:180
  268.9 126.2 %reduce-scatter.17.cloned.1.call-start = ((), (), s32[]{:S(2)}) async-start(), calls=%async_computation.15 | async-start | bytes 1966080 | tf_op jit(solution)/shard_map/reduce_scatter | solution.py:180
  274.2 120.9 %copy-start.44 = (f32[768]{0:T(1024)S(1)}, f32[768]{0:T(1024)}, u32[]{:S(2)}) copy-start(f32[768]{0:T(1024)} %param.33) | copy-start | bytes 9220
  274.2 120.9 %copy-start.47 = (f32[256]{0:T(256)S(1)}, f32[256]{0:T(256)}, u32[]{:S(2)}) copy-start(f32[256]{0:T(256)} %copy-done.46) | copy-start | bytes 3076
  274.2 120.9 %copy-start.49 = (f32[256]{0:T(256)S(1)}, f32[256]{0:T(256)}, u32[]{:S(2)}) copy-start(f32[256]{0:T(256)} %copy-done.48) | copy-start | bytes 3076
  274.3 145.6 %all-gather.21.cloned.1.call-start = ((), (), s32[]{:S(2)}) async-start(), calls=%async_computation.24 | async-start | bytes 1966080 | tf_op jit(solution)/shard_map/all_gather | solution.py:227
  400.1 53.7 %all-gather.19.cloned.1.call-start = ((), (), s32[]{:S(2)}) async-start(), calls=%async_computation.21 | async-start | bytes 1966080 | tf_op jit(solution)/shard_map/all_gather | solution.py:227
  400.7 156.4 %reduce-scatter.37.cloned.1.call-start = ((), (), s32[]{:S(2)}) async-start(), calls=%async_computation.31 | async-start | bytes 884736
  493.2 133.2 %reduce-scatter.31.cloned.1.call-start = ((), (), s32[]{:S(2)}) async-start(), calls=%async_computation.26 | async-start | bytes 2211840 | tf_op jit(solution)/shard_map/reduce_scatter | solution.py:275
  500.9 164.7 %reduce-scatter.25.cloned.1.call-start = ((), (), s32[]{:S(2)}) async-start(), calls=%async_computation.22 | async-start | bytes 3932160 | tf_op jit(solution)/shard_map/reduce_scatter | solution.py:253
  505.4 200.5 %reduce-scatter.29.cloned.1.call-start = ((), (), s32[]{:S(2)}) async-start(), calls=%async_computation.25 | async-start | bytes 3932160 | tf_op jit(solution)/shard_map/reduce_scatter | solution.py:253
  509.8 270.4 %reduce-scatter.35.cloned.1.call-start = ((), (), s32[]{:S(2)}) async-start(), calls=%async_computation.28 | async-start | bytes 2654208 | tf_op jit(solution)/shard_map/reduce_scatter | solution.py:278
  518.6 334.3 %reduce-scatter.33.cloned.1.call-start = ((), (), s32[]{:S(2)}) async-start(), calls=%async_computation.27 | async-start | bytes 2654208 | tf_op jit(solution)/shard_map/reduce_scatter | solution.py:277
  524.9 181.1 %copy-start.3 = (bf16[2,256,1,768]{3,1,2,0:T(8,128)(2,1)S(1)}, bf16[2,256,1,768]{3,1,2,0:T(8,128)(2,1)}, u32[]{:S(2)}) copy-start(bf16[2,256,1,768]{3,1,2,0:T(8,128)(2,1)} %param.24) | copy-start | bytes 2359300
  524.9 181.1 %copy-start.45 = (f32[768]{0:T(1024)S(1)}, f32[768]{0:T(1024)}, u32[]{:S(2)}) copy-start(f32[768]{0:T(1024)} %param.27) | copy-start | bytes 9220
  524.9 181.1 %copy-start.51 = (f32[256]{0:T(256)S(1)}, f32[256]{0:T(256)}, u32[]{:S(2)}) copy-start(f32[256]{0:T(256)} %copy-done.50) | copy-start | bytes 3076
  524.9 181.1 %copy-start.53 = (f32[256]{0:T(256)S(1)}, f32[256]{0:T(256)}, u32[]{:S(2)}) copy-start(f32[256]{0:T(256)} %copy-done.52) | copy-start | bytes 3076
  524.9 181.0 %copy-start.55 = (f32[256]{0:T(256)S(1)}, f32[256]{0:T(256)}, u32[]{:S(2)}) copy-start(f32[256]{0:T(256)} %copy-done.54) | copy-start | bytes 3076
  525.1 183.1 %copy-start.21 = (f32[256,1,768]{2,0,1:T(8,128)S(1)}, f32[256,1,768]{2,0,1:T(8,128)}, u32[]{:S(2)}) copy-start(f32[256,1,768]{2,0,1:T(8,128)} %get-tuple-element.611) | copy-start | bytes 2359300
  525.1 183.1 %copy-start.22 = (f32[256,1,768]{2,0,1:T(8,128)S(1)}, f32[256,1,768]{2,0,1:T(8,128)}, u32[]{:S(2)}) copy-start(f32[256,1,768]{2,0,1:T(8,128)} %get-tuple-element.634) | copy-start | bytes 2359300
  710.1 142.8 %copy-start.1 = (bf16[768,768]{1,0:T(8,128)(2,1)S(1)}, bf16[768,768]{1,0:T(8,128)(2,1)}, u32[]{:S(2)}) copy-start(bf16[768,768]{1,0:T(8,128)(2,1)} %param.37) | copy-start | bytes 3538948
  (84 other events, 1025.8 us)
Sparse Core Ops, SparseCore 0:
  12.8 22.3 all-gather.14
  37.3 19.6 all-gather.10
  86.8 37.8 reduce-scatter.18
  127.1 37.8 reduce-scatter.14
  169.1 19.6 all-gather.16
  190.1 19.6 all-gather.24
  211.9 19.6 all-gather.12
  233.2 19.6 all-gather.22
  255.4 37.8 reduce-scatter.26
  295.7 37.8 reduce-scatter.22
  336.7 27.9 reduce-scatter.20
  367.1 27.9 reduce-scatter.16
  400.2 19.5 all-gather.20
  421.3 19.6 all-gather.18
  493.3 63.1 reduce-scatter.36
  559.9 66.4 reduce-scatter.30
  628.8 36.7 reduce-scatter.24
  668.0 37.8 reduce-scatter.28
  710.0 70.0 reduce-scatter.34
  784.1 68.8 reduce-scatter.32
where the time goes:
time: 868 us; the launch traced here: 860 us
  waiting for transfers between devices  535 us (62%)
  matrix products  132 us (15%)
  blocking collectives  62.9 us (7%)
  other arithmetic  57.5 us (7%)
  local copies, waits for them, and re-layouts  38.8 us (4%)
  loops' own time  16 us (2%)
  between operations  15.5 us (2%)
    reduce_scatter x2, waiting for transfers between devices, body(): lax.psum_scatter(jnp.einsum('lse,de->lsd', grad_joined_rows, w_joined, pr...  77.5 us
    reduce_scatter x1, waiting for transfers between devices, body(): lax.psum_scatter(totals[2], 'dp', scatter_dimension=0, tiled=True)  72.8 us
    reduce_scatter x1, waiting for transfers between devices, body(): lax.psum_scatter(totals[0], 'dp', scatter_dimension=0, tiled=True)  67.7 us
    reduce_scatter x2, waiting for transfers between devices, body(): lax.psum_scatter(jnp.einsum('pav,zv->paz', upper_branch_gradient, up_weig...  59.2 us
    reduce_scatter x2, waiting for transfers between devices, body(): lax.psum_scatter(jnp.einsum('pxm,mk->pxk', hidden_reduced_precision, down...  58.6 us
    reduce_scatter x2, waiting for transfers between devices, body(): lax.psum_scatter(jnp.einsum('grn,nd->grd', mixed_reduced_precision, outpu...  51.2 us
    psum x1, blocking collectives, body(): lax.psum((small[0], small[1], small[2], small[3], small[4], small[5]), ('...  40.7 us
    all_gather x2, waiting for transfers between devices, body(): lax.all_gather(normed.astype(jnp.bfloat16), 'tensor', axis=0, tiled=True)  38.8 us
  transfers between devices with their start and end apart: 20, of which 18 were waited for; matrix products, arithmetic and copies ran while one was open for 17% of the time, Pallas kernels for 0%

commit v1 on v0

v1 whole, which is shorter than its diff:
```python
import functools

import jax
import jax.numpy as jnp
from jax import lax
from jax.experimental import pallas as pl
from jax.experimental.pallas import tpu as pltpu
from jax.sharding import PartitionSpec as P

HEAD_DIM = 64
EPS = 1e-06
MASKED = -1e30
SELF_CODE = 4096.0
F32 = jnp.float32
BF16 = jnp.bfloat16
MESH = pl.DeviceIdType.MESH
GELU_A = 0.7978845608028654
GELU_B = 0.044715


def mm(a, b):
    return lax.dot_general(a, b, (((1,), (0,)), ((), ())), preferred_element_type=F32)


def mm_nt(a, b):
    return lax.dot_general(a, b, (((1,), (1,)), ((), ())), preferred_element_type=F32)


def mm_tn(a, b):
    return lax.dot_general(a, b, (((0,), (0,)), ((), ())), preferred_element_type=F32)


def mm_tt(a, b):
    return lax.dot_general(a, b, (((0,), (1,)), ((), ())), preferred_element_type=F32)


def norm_parts(v):
    mean = jnp.mean(v, axis=-1, keepdims=True)
    cen = v - mean
    r = lax.rsqrt(jnp.mean(cen * cen, axis=-1, keepdims=True) + EPS)
    return cen * r, r


def norm_back(e, n, r):
    first = jnp.mean(e, axis=-1, keepdims=True)
    second = jnp.mean(e * n, axis=-1, keepdims=True)
    return r * (e - first - n * second)


class Names:
    def __init__(self, send, recv):
        self.send, self.recv, self.used = send, recv, 0

    def copy(self, src, dst, device):
        i = self.used
        self.used += 1
        return pltpu.make_async_remote_copy(
            src_ref=src,
            dst_ref=dst,
            send_sem=self.send.at[i],
            recv_sem=self.recv.at[i],
            device_id=device,
            device_id_type=MESH,
        )


SEMS = 120


def block_kernel(
    n_dp,
    in_dp,
    x_ref,
    g_ref,
    seg_ref,
    val_ref,
    gain1,
    shift1,
    bias_qv,
    bias_out,
    gain2,
    shift2,
    bias_up,
    bias_down,
    wqkv_hbm,
    wo_hbm,
    wu_hbm,
    wd_hbm,
    out_ref,
    gtok_ref,
    small_ref,
    qvb_ref,
    own_a,
    own_b,
    wq,
    wo,
    wu,
    wd,
    a_all,
    c_all,
    g_all,
    d_all,
    qT,
    kT,
    vT,
    kk,
    vv,
    oT,
    lse,
    doT,
    h_scr,
    du_scr,
    kcol,
    bias_scr,
    s_scr,
    p_scr,
    ds_scr,
    dkT,
    dvT,
    dqkvT,
    part,
    crecv,
    ysend,
    yrecv,
    mid,
    ga,
    gb,
    *rest,
):
    if in_dp:
        xs_a, xr_a, zr_a, xs_b, xr_b, zr_b, vec, trecv, dsend, drecv, send_sem, recv_sem, w_sem = rest
    else:
        vec, send_sem, recv_sem, w_sem = rest
    micro, R, D = x_ref.shape
    L = 4 * R
    HL = wo.shape[0]
    FL = wu.shape[1]
    heads = HL // HEAD_DIM
    scale = HEAD_DIM ** (-0.5)
    t = lax.axis_index("tensor")
    dp = lax.axis_index("dp")
    t_core = t + 1 - 2 * lax.rem(t, 2)
    t_y = lax.rem(t + 2, 4)
    t_diag = t_core + 2 - 4 * (t_core // 2)
    blocks = (t, t_core, t_y, t_diag)
    core = {"tensor": t_core}
    ydev = {"tensor": t_y}
    names = Names(send_sem, recv_sem)

    barrier = pltpu.get_barrier_semaphore()
    met = 0
    for dev in (t_core, t_y, t_diag):
        pl.semaphore_signal(barrier, inc=1, device_id={"tensor": dev}, device_id_type=MESH)
        met += 1
    if in_dp:
        for off in range(1, n_dp):
            pl.semaphore_signal(barrier, inc=1, device_id={"dp": lax.rem(dp + off, n_dp)}, device_id_type=MESH)
            met += 1
    loads = [
        pltpu.make_async_copy(s, d, w_sem.at[i])
        for i, (s, d) in enumerate(((wqkv_hbm, wq), (wo_hbm, wo), (wu_hbm, wu), (wd_hbm, wd)))
    ]
    for ld in loads:
        ld.start()

    CH = min(64, R)
    KC = min(128, R)

    half = R // 2

    class Gather:
        def __init__(self, buf, m):
            b = self.b = buf
            self.core = names.copy(b.at[m, 0], b.at[m, 1], core)
            self.y = [names.copy(b.at[m, 0, pl.ds(i * half, half)], b.at[m, 2, pl.ds(i * half, half)], ydev) for i in range(2)]
            self.fwd = [names.copy(b.at[m, 2, pl.ds(i * half, half)], b.at[m, 3, pl.ds(i * half, half)], core) for i in range(2)]

        def start_core(self):
            self.core.start()

        def start_y(self):
            for c in self.y:
                c.start()

        def wait_core(self):
            self.core.wait_recv()

        def forward(self):
            for c, f in zip(self.y, self.fwd):
                c.wait_recv()
                f.start()

        def wait_last(self):
            for f in self.fwd:
                f.wait_recv()

        def drain(self):
            for c in [self.core] + self.y + self.fwd:
                c.wait_send()

    class Scatter:
        def __init__(self, p):
            self.p = p
            self.c3 = names.copy(part.at[p, 3], crecv.at[p, 1], core)
            self.c1 = names.copy(part.at[p, 1], crecv.at[p, 0], core)
            self.y = names.copy(ysend.at[p], yrecv.at[p], ydev)

        def start_far(self):
            self.c3.start()

        def start_near(self):
            self.c1.start()

        def relay(self):
            p = self.p
            self.c3.wait_recv()

            @pl.loop(0, R // CH)
            def _(i):
                rows = pl.ds(pl.multiple_of(i * CH, CH), CH)
                ysend[p, rows, :] = (part[p, 2, rows, :].astype(F32) + crecv[p, 1, rows, :].astype(F32)).astype(BF16)

            self.y.start()

        def arrive(self):
            self.c1.wait_recv()
            self.y.wait_recv()

        def total(self, rows):
            p = self.p
            return part[p, 0, rows, :].astype(F32) + crecv[p, 0, rows, :].astype(F32) + yrecv[p, rows, :].astype(F32)

        def drain(self):
            for c in (self.c3, self.c1, self.y):
                c.wait_send()

    def by_rows(step):
        @pl.loop(0, R // CH)
        def _(i):
            step(pl.ds(pl.multiple_of(i * CH, CH), CH))

    ag_a = [Gather(a_all, m) for m in range(micro)]
    ag_c = [Gather(c_all, m) for m in range(micro)]
    ag_g = [Gather(g_all, m) for m in range(micro)]
    ag_d = [Gather(d_all, m) for m in range(micro)]
    rs_attn = [Scatter(m) for m in range(micro)]
    rs_branch = [Scatter(m) for m in range(micro)]
    rs_dc = [Scatter(micro + m) for m in range(micro)]
    rs_da = [Scatter(micro + m) for m in range(micro)]

    def first_norm(m):
        def step(rows):
            n, _ = norm_parts(x_ref[m, rows, :].astype(F32))
            a_all[m, 0, rows, :] = (n * gain1[...] + shift1[...]).astype(BF16)

        by_rows(step)

    def codes(m):
        for r in range(4):
            seg = seg_ref[pl.ds(m, 1), pl.ds(pl.multiple_of(blocks[r] * R, R), R)].astype(F32)
            val = val_ref[pl.ds(m, 1), pl.ds(pl.multiple_of(blocks[r] * R, R), R)]
            place = lax.broadcasted_iota(jnp.int32, (1, R), 1).astype(F32) + (SELF_CODE + r * R)
            code = jnp.where(val > 0, seg, place)
            kcol[pl.ds(r * R, R), :] = jnp.broadcast_to(code, (128, R)).T

    def qkv(m):
        def slot(r):
            a = a_all[m, r]
            cols = slice(r * R, (r + 1) * R)
            allT = mm_nt(wq[...], a)
            bq = bias_qv[0].reshape(HL, 1)
            bv = bias_qv[1].reshape(HL, 1)
            q_low = (allT[:HL] + bq).astype(BF16)
            qT[m, :, cols] = q_low * jnp.asarray(scale, BF16)
            kT[m, :, cols] = allT[HL : 2 * HL].astype(BF16)
            vT[m, :, cols] = (allT[2 * HL :] + bv).astype(BF16)
            kv = mm_nt(a, wq[HL:, :])
            for h in range(heads):
                kk[m, h, cols, :] = kv[:, h * HEAD_DIM : (h + 1) * HEAD_DIM].astype(BF16)
                bv_row = jnp.broadcast_to(bv, (HL, 128)).T[:1, h * HEAD_DIM : (h + 1) * HEAD_DIM]
                vv[m, h, cols, :] = (kv[:, HL + h * HEAD_DIM : HL + (h + 1) * HEAD_DIM] + bv_row).astype(BF16)

        slot(0)
        ag_a[m].wait_core()
        slot(1)
        ag_a[m].forward()
        slot(2)
        ag_a[m].wait_last()
        slot(3)

    def mask_block(m, qb):
        cols = pl.ds(pl.multiple_of(qb * R, R), R)
        place = (lax.broadcasted_iota(jnp.int32, (1, R), 1) + qb * R).astype(F32) + SELF_CODE
        blk = jnp.where(qb == 0, blocks[0], jnp.where(qb == 1, blocks[1], jnp.where(qb == 2, blocks[2], blocks[3])))
        seg = seg_ref[pl.ds(m, 1), pl.ds(pl.multiple_of(blk * R, R), R)].astype(F32)
        for c in range(L // KC):
            kc = kcol[c * KC : (c + 1) * KC, :1]
            ok = (kc == seg) | (kc == place)
            bias_scr[c * KC : (c + 1) * KC, :] = jnp.where(ok, 0.0, MASKED)
        return cols

    def fold8(v, op):
        out = v[:8]
        for i in range(1, v.shape[0] // 8):
            out = op(out, v[i * 8 : (i + 1) * 8])
        return out

    def attend(m):
        @pl.loop(0, 4)
        def _(qb):
            cols = mask_block(m, qb)

            @pl.loop(0, heads)
            def _(h):
                hrows = pl.ds(pl.multiple_of(h * HEAD_DIM, HEAD_DIM), HEAD_DIM)
                q = qT[m, hrows, cols]
                top8 = None
                for c in range(L // KC):
                    rows = slice(c * KC, (c + 1) * KC)
                    s = mm(kk[m, h, rows, :], q) + bias_scr[rows, :]
                    s_scr[rows, :] = s
                    part8 = fold8(s, jnp.maximum)
                    top8 = part8 if top8 is None else jnp.maximum(top8, part8)
                top = jnp.max(top8, axis=0, keepdims=True)
                sum8 = None
                for c in range(L // KC):
                    rows = slice(c * KC, (c + 1) * KC)
                    p = jnp.exp(s_scr[rows, :] - top)
                    p_scr[rows, :] = p.astype(BF16)
                    part8 = fold8(p, jnp.add)
                    sum8 = part8 if sum8 is None else sum8 + part8
                total = jnp.sum(sum8, axis=0, keepdims=True)
                o = mm(vT[m, hrows, :], p_scr[...])
                oT[m, hrows, cols] = (o / total).astype(BF16)
                lse[m, pl.ds(h, 1), cols] = top + jnp.log(total)

    def attn_out(m):
        rs = rs_attn[m]
        for r in (3, 2, 1, 0):
            part[m, r] = mm_tn(oT[m, :, r * R : (r + 1) * R], wo[...]).astype(BF16)
            if r == 3:
                rs.start_far()
            if r == 1:
                rs.start_near()
                rs.relay()

    def middle(m):
        rs_attn[m].arrive()

        def step(rows):
            v = x_ref[m, rows, :].astype(F32) + (rs_attn[m].total(rows) + bias_out[...])
            mid[m, rows, :] = v
            n, _ = norm_parts(v)
            c_all[m, 0, rows, :] = (n * gain2[...] + shift2[...]).astype(BF16)

        by_rows(step)
        ag_c[m].start_core()
        ag_c[m].start_y()

    def feed(m, first):
        @pl.loop(first, first + 2)
        def _(r):
            rows = pl.ds(pl.multiple_of(r * R, R), R)
            g = g_all[m, r]
            u = mm(c_all[m, r], wu[...]) + bias_up[...]
            dh = mm_nt(g, wd[...])
            th = jnp.tanh(GELU_A * (u + GELU_B * (u * u * u)))
            half_u = 0.5 * (1.0 + th)
            slope = half_u + (0.5 * u) * (1.0 - th * th) * (GELU_A * (1.0 + (3.0 * GELU_B) * (u * u)))
            hid = (u * half_u).astype(BF16)
            du = (dh * slope).astype(BF16)
            h_scr[rows, :] = hid
            du_scr[rows, :] = du
            vec[6:7, :FL] += jnp.sum(du.astype(F32), axis=0, keepdims=True)
            part[micro + m, r] = mm_nt(du, wu[...]).astype(BF16)
            part[m, r] = mm(hid, wd[...]).astype(BF16)

    def weight_sums(m):
        B = min(256, D)

        @pl.loop(0, D // B)
        def _(i):
            f = pl.ds(pl.multiple_of(i * B, B), B)
            for r in range(4):
                down = mm_tn(g_all[m, r, :, f], h_scr[r * R : (r + 1) * R, :])
                up = mm_tn(c_all[m, r, :, f], du_scr[r * R : (r + 1) * R, :])
                if m == 0 and r == 0:
                    ga[f, :FL] = down
                    ga[f, FL:] = up
                else:
                    ga[f, :FL] += down
                    ga[f, FL:] += up

    def add_row(i, v):
        vec[i : i + 1, :] += jnp.sum(v, axis=0, keepdims=True)

    def turn(m):
        rs_dc[m].arrive()

        def step(rows):
            dc = rs_dc[m].total(rows)
            n, r = norm_parts(mid[m, rows, :])
            add_row(3, dc * n)
            add_row(4, dc)
            g = g_ref[m, rows, :].astype(F32)
            add_row(5, g)
            dx = g + norm_back(dc * gain2[...], n, r)
            gtok_ref[m, rows, :] = dx
            low = dx.astype(BF16)
            add_row(2, low.astype(F32))
            d_all[m, 0, rows, :] = low

        by_rows(step)
        ag_d[m].start_core()
        ag_d[m].start_y()

    def attend_back(m):
        def project(r):
            doT[:, r * R : (r + 1) * R] = mm_nt(wo[...], d_all[m, r]).astype(BF16)

        project(0)
        ag_d[m].wait_core()
        project(1)
        ag_d[m].forward()
        project(2)
        ag_d[m].wait_last()
        project(3)
        dkT[...] = jnp.zeros_like(dkT)
        dvT[...] = jnp.zeros_like(dvT)

        @pl.loop(0, 4)
        def _(qb):
            cols = mask_block(m, qb)

            @pl.loop(0, heads)
            def _(h):
                hrows = pl.ds(pl.multiple_of(h * HEAD_DIM, HEAD_DIM), HEAD_DIM)
                q = qT[m, hrows, cols]
                do = doT[hrows, cols]
                inner = jnp.sum(do.astype(F32) * oT[m, hrows, cols].astype(F32), axis=0, keepdims=True)
                log_total = lse[m, pl.ds(h, 1), cols]
                for c in range(L // KC):
                    rows = slice(c * KC, (c + 1) * KC)
                    s = mm(kk[m, h, rows, :], q) + bias_scr[rows, :]
                    p = jnp.exp(s - log_total)
                    dprob = mm(vv[m, h, rows, :], do)
                    p_scr[rows, :] = p.astype(BF16)
                    ds_scr[rows, :] = (p * (dprob - inner)).astype(BF16)
                dvT[hrows, :] += mm_nt(do, p_scr[...])
                dkT[hrows, :] += mm_nt(q, ds_scr[...])
                dqkvT[hrows, cols] = (mm(kT[m, hrows, :], ds_scr[...]) * scale).astype(BF16)

        dqkvT[HL : 2 * HL, :] = dkT[...].astype(BF16)
        dqkvT[2 * HL :, :] = dvT[...].astype(BF16)
        rs = rs_da[m]
        for r in (3, 2, 1, 0):
            part[micro + m, r] = mm_tn(dqkvT[:, r * R : (r + 1) * R], wq[...]).astype(BF16)
            if r == 3:
                rs.start_far()
            if r == 1:
                rs.start_near()
                rs.relay()

    def head_sums(m):
        B = min(256, D)
        sums = mm_nt(jnp.ones((8, L), BF16), dqkvT[...])[:1]
        if m == 0:
            qvb_ref[...] = sums
        else:
            qvb_ref[...] += sums

        @pl.loop(0, D // B)
        def _(i):
            f = pl.ds(pl.multiple_of(i * B, B), B)
            for r in range(4):
                cols = slice(r * R, (r + 1) * R)
                j = mm_tt(a_all[m, r, :, f], dqkvT[:, cols])
                o = mm_tt(d_all[m, r, :, f], oT[m, :, cols])
                if m == 0 and r == 0:
                    gb[f, : 3 * HL] = j
                    gb[f, 3 * HL :] = o
                else:
                    gb[f, : 3 * HL] += j
                    gb[f, 3 * HL :] += o

    def finish_out(m):
        rs_branch[m].arrive()

        def step(rows):
            out_ref[m, rows, :] = (mid[m, rows, :] + (rs_branch[m].total(rows) + bias_down[...])).astype(BF16)

        by_rows(step)

    def finish_in(m):
        rs_da[m].arrive()

        def step(rows):
            da = rs_da[m].total(rows)
            n, r = norm_parts(x_ref[m, rows, :].astype(F32))
            add_row(0, da * n)
            add_row(1, da)
            gtok_ref[m, rows, :] += norm_back(da * gain1[...], n, r)

        by_rows(step)

    class Reduce:
        def __init__(self, acc, xs, xr, zr, own):
            self.acc, self.xs, self.xr, self.zr, self.own = acc, xs, xr, zr, own
            self.rows = D // n_dp
            self.n2 = n_dp // 2
            self.px = lax.rem(dp, 2)
            self.pz = dp // 2
            self.x = names.copy(xs, xr, {"dp": dp + 1 - 2 * self.px})
            self.z = []
            for off in range(1, self.n2):
                to = lax.rem(self.pz + off, self.n2)
                self.z.append(names.copy(xs.at[off - 1], zr.at[off - 1], {"dp": 2 * to + self.px}))

        def at(self, z, px):
            n = self.rows
            return pl.ds(pl.multiple_of((2 * z + px) * n, n), n)

        def start(self):
            for z in range(self.n2):
                self.xs[z] = self.acc[self.at(z, 1 - self.px), :].astype(BF16)
            self.x.start()

        def second(self):
            self.x.wait_send()
            self.x.wait_recv()
            for off in range(1, self.n2):
                to = lax.rem(self.pz + off, self.n2)
                self.xs[off - 1] = (self.acc[self.at(to, self.px), :] + self.xr[to].astype(F32)).astype(BF16)
                self.z[off - 1].start()

        def last(self):
            tot = self.acc[self.at(self.pz, self.px), :] + self.xr[self.pz].astype(F32)
            for off in range(1, self.n2):
                self.z[off - 1].wait_recv()
                tot = tot + self.zr[off - 1].astype(F32)
            self.own[...] = tot

        def drain(self):
            for c in self.z:
                c.wait_send()

    if in_dp:
        red_a = Reduce(ga, xs_a, xr_a, zr_a, own_a)
        red_b = Reduce(gb, xs_b, xr_b, zr_b, own_b)
        small_t = [names.copy(vec, trecv.at[i], {"tensor": d}) for i, d in enumerate((t_core, t_y, t_diag))]
        small_d = [names.copy(dsend, drecv.at[off - 1], {"dp": lax.rem(dp + off, n_dp)}) for off in range(1, n_dp)]

    vec[...] = jnp.zeros_like(vec)
    for m in range(micro):
        g_all[m, 0] = g_ref[m]
    first_norm(0)
    pl.semaphore_wait(barrier, met)
    ag_a[0].start_core()
    ag_a[0].start_y()
    for m in range(1, micro):
        first_norm(m)
        ag_a[m].start_core()
        ag_a[m].start_y()
    for m in range(micro):
        ag_g[m].start_core()
    ag_g[0].start_y()
    codes(0)
    loads[0].wait()
    loads[1].wait()

    qkv(0)
    attend(0)
    attn_out(0)
    codes(1)
    qkv(1)
    attend(1)
    middle(0)
    attn_out(1)
    ag_g[1].start_y()
    loads[2].wait()
    loads[3].wait()

    def feed_all(m, between):
        ag_c[m].wait_core()
        ag_g[m].wait_core()
        rs_attn[m].drain()
        feed(m, 0)
        between()
        ag_c[m].forward()
        ag_g[m].forward()
        ag_c[m].wait_last()
        ag_g[m].wait_last()
        feed(m, 2)
        rs_dc[m].start_far()
        rs_dc[m].start_near()
        rs_dc[m].relay()
        rs_branch[m].start_far()
        rs_branch[m].start_near()
        rs_branch[m].relay()
        weight_sums(m)

    feed_all(0, lambda: middle(1))
    feed_all(1, lambda: turn(0))
    if in_dp:
        red_a.start()
    turn(1)
    codes(0)
    rs_dc[0].drain()
    attend_back(0)
    head_sums(0)
    finish_out(0)
    finish_out(1)
    if in_dp:
        red_a.second()
    codes(1)
    rs_dc[1].drain()
    attend_back(1)
    head_sums(1)
    if in_dp:
        red_b.start()
        red_a.last()
    finish_in(0)
    finish_in(1)
    if in_dp:
        red_b.second()
        vec[7:8, : 3 * HL] = qvb_ref[...]
        for c in small_t:
            c.start()
        for c in small_t:
            c.wait_recv()
        six = lax.broadcasted_iota(jnp.int32, vec.shape, 0) < 6
        dsend[...] = vec[...] + jnp.where(six, trecv[0] + trecv[1] + trecv[2], 0.0)
        for c in small_d:
            c.start()
        red_b.last()
        tot = dsend[...]
        for i, c in enumerate(small_d):
            c.wait_recv()
            tot = tot + drecv[i]
        small_ref[...] = tot
        for c in small_t + small_d:
            c.wait_send()
        red_a.drain()
        red_b.drain()
    else:
        small_ref[...] = vec[...]
        own_a[...] = ga[...]
        own_b[...] = gb[...]
    for m in range(micro):
        rs_branch[m].drain()
        rs_da[m].drain()
        for gather in (ag_a, ag_c, ag_g, ag_d):
            gather[m].drain()


def body(
    n_dp,
    tokens,
    segment_ids,
    valid_mask,
    gain_one,
    shift_one,
    w_qkv,
    bias_qv,
    output_weight,
    bias_out,
    gain_two,
    shift_two,
    up_weight,
    bias_up,
    down_weight,
    bias_down,
    out_grad,
):
    micro, R, _, D = tokens.shape
    L = 4 * R
    HL = w_qkv.shape[2]
    FL = up_weight.shape[1]
    heads = HL // HEAD_DIM
    in_dp = n_dp > 1 and n_dp % 2 == 0 and D % n_dp == 0 and (D // n_dp) % 16 == 0
    n2, rows = n_dp // 2, D // n_dp
    row = lambda v: v.reshape(1, -1)
    wqT = jnp.transpose(w_qkv, (1, 2, 0)).reshape(3 * HL, D)
    vmem = pl.BlockSpec(memory_space=pltpu.VMEM)
    hbm = pl.BlockSpec(memory_space=pl.ANY)
    own_rows = rows if in_dp else D
    ca, cb = 2 * FL, 4 * HL
    scratch = [
        pltpu.VMEM((3 * HL, D), BF16),
        pltpu.VMEM((HL, D), BF16),
        pltpu.VMEM((D, FL), BF16),
        pltpu.VMEM((FL, D), BF16),
        pltpu.VMEM((micro, 4, R, D), BF16),
        pltpu.VMEM((micro, 4, R, D), BF16),
        pltpu.VMEM((micro, 4, R, D), BF16),
        pltpu.VMEM((micro, 4, R, D), BF16),
        pltpu.VMEM((micro, HL, L), BF16),
        pltpu.VMEM((micro, HL, L), BF16),
        pltpu.VMEM((micro, HL, L), BF16),
        pltpu.VMEM((micro, heads, L, HEAD_DIM), BF16),
        pltpu.VMEM((micro, heads, L, HEAD_DIM), BF16),
        pltpu.VMEM((micro, HL, L), BF16),
        pltpu.VMEM((micro, heads, L), F32),
        pltpu.VMEM((HL, L), BF16),
        pltpu.VMEM((L, FL), BF16),
        pltpu.VMEM((L, FL), BF16),
        pltpu.VMEM((L, 128), F32),
        pltpu.VMEM((L, R), F32),
        pltpu.VMEM((L, R), F32),
        pltpu.VMEM((L, R), BF16),
        pltpu.VMEM((L, R), BF16),
        pltpu.VMEM((HL, L), F32),
        pltpu.VMEM((HL, L), F32),
        pltpu.VMEM((3 * HL, L), BF16),
        pltpu.VMEM((2 * micro, 4, R, D), BF16),
        pltpu.VMEM((2 * micro, 2, R, D), BF16),
        pltpu.VMEM((2 * micro, R, D), BF16),
        pltpu.VMEM((2 * micro, R, D), BF16),
        pltpu.VMEM((micro, R, D), F32),
        pltpu.VMEM((D, ca), F32),
        pltpu.VMEM((D, cb), F32),
    ]
    if in_dp:
        for c in (ca, cb):
            scratch += [
                pltpu.VMEM((n2, rows, c), BF16),
                pltpu.VMEM((n2, rows, c), BF16),
                pltpu.VMEM((n2 - 1, rows, c), BF16),
            ]
    scratch += [pltpu.VMEM((8, D), F32)]
    if in_dp:
        scratch += [pltpu.VMEM((3, 8, D), F32), pltpu.VMEM((8, D), F32), pltpu.VMEM((n_dp - 1, 8, D), F32)]
    scratch += [pltpu.SemaphoreType.DMA((SEMS,)), pltpu.SemaphoreType.DMA((SEMS,)), pltpu.SemaphoreType.DMA((4,))]
    outs = pl.pallas_call(
        functools.partial(block_kernel, n_dp, in_dp),
        out_shape=(
            jax.ShapeDtypeStruct((micro, R, D), BF16),
            jax.ShapeDtypeStruct((micro, R, D), F32),
            jax.ShapeDtypeStruct((8, D), F32),
            jax.ShapeDtypeStruct((1, 3 * HL), F32),
            jax.ShapeDtypeStruct((own_rows, ca), F32),
            jax.ShapeDtypeStruct((own_rows, cb), F32),
        ),
        in_specs=[vmem] * 12 + [hbm] * 4,
        out_specs=[vmem] * 6,
        scratch_shapes=scratch,
        compiler_params=pltpu.CompilerParams(
            collective_id=0, has_side_effects=True, vmem_limit_bytes=67043328
        ),
        name="vision_block",
    )(
        tokens.reshape(micro, R, D),
        out_grad.reshape(micro, R, D),
        segment_ids.reshape(micro, L),
        valid_mask.reshape(micro, L),
        row(gain_one),
        row(shift_one),
        bias_qv.reshape(2, HL, 1),
        row(bias_out),
        row(gain_two),
        row(shift_two),
        row(bias_up),
        row(bias_down),
        wqT,
        output_weight,
        up_weight,
        down_weight,
    )
    out, gtok, small, qvb, share_a, share_b = outs
    if not in_dp:
        share_a, share_b = (lax.psum_scatter(v, "dp", scatter_dimension=0, tiled=True) for v in (share_a, share_b))
        small = jnp.concatenate([lax.psum(small[:6], ("dp", "tensor")), lax.psum(small[6:7], "dp")])
        sums = lax.psum(qvb[0], "dp")
    else:
        sums = small[7, : 3 * HL]
    own_rows = share_a.shape[0]
    grad_qkv = share_b[:, : 3 * HL].reshape(own_rows, 3, HL)
    grad_bias_qv = jnp.stack([sums[:HL], sums[2 * HL :]])
    return (
        out.reshape(micro, R, 1, D),
        gtok.reshape(micro, R, 1, D),
        small[0],
        small[1],
        grad_qkv,
        grad_bias_qv,
        share_b[:, 3 * HL :].T,
        small[2],
        small[3],
        small[4],
        share_a[:, FL:],
        small[6, :FL],
        share_a[:, :FL].T,
        small[5],
    )


def solution(mesh):
    placed = (
        P(None, "tensor", "dp", None),
        P(None, "dp", None),
        P(None, "dp", None),
        P(),
        P(),
        P(None, None, "tensor"),
        P(None, "tensor"),
        P("tensor", None),
        P(),
        P(),
        P(),
        P(None, "tensor"),
        P("tensor"),
        P("tensor", None),
        P(),
        P(None, "tensor", "dp", None),
    )
    return jax.shard_map(
        functools.partial(body, mesh.shape["dp"]),
        mesh=mesh,
        in_specs=placed,
        out_specs=(
            P(None, "tensor", "dp", None),
            P(None, "tensor", "dp", None),
            P(),
            P(),
            P("dp", None, "tensor"),
            P(None, "tensor"),
            P("tensor", "dp"),
            P(),
            P(),
            P(),
            P("dp", "tensor"),
            P("tensor"),
            P("tensor", "dp"),
            P(),
        ),
        check_vma=False,
    )
```

time: 868 us -> 212 us (0.24)
  waiting for transfers between devices: 535 us -> 0 us
  Pallas kernels: 0 us -> 190 us
  matrix products: 132 us -> 0 us
  blocking collectives: 62.9 us -> 0 us
  other arithmetic: 57.5 us -> 0.59 us
  local copies, waits for them, and re-layouts: 38.8 us -> 20.2 us
  loops' own time: 16 us -> 0 us
  between operations: 15.5 us -> 0.7 us
    reduce_scatter x11 -> x0, waiting for transfers between devices: 413 us -> none  [the longest x2 77.5 us: body(): lax.psum_scatter(jnp.einsum('lse,de->lsd', grad_joined_rows, w_joined, pr...]
    pallas_call x0 -> x1, Pallas kernels: none -> 190 us  [body(): pl.pallas_call(functools.partial(block_kernel, n_dp, in_dp), out_shape=(j...]
    dot_general x52 -> x0, matrix products: 132 us -> none  [the longest x2 12.5 us: body(): jnp.einsum('hci,gi->hcg', gathered_gradient, down_weight, preferred_eleme...]
    all_gather x8 -> x0, waiting for transfers between devices: 118 us -> none  [the longest x2 38.8 us: body(): lax.all_gather(normed.astype(jnp.bfloat16), 'tensor', axis=0, tiled=True)]
    psum x2 -> x0, blocking collectives: 62.9 us -> none  [the longest x1 40.7 us: body(): lax.psum((small[0], small[1], small[2], small[3], small[4], small[5]), ('...]
    reduce_sum x17 -> x0, other arithmetic: 24.1 us -> none  [the longest x4 7.22 us: block_step(): total = jnp.sum(jnp.exp(scores - top), axis=-1, keepdims=True)]
    another operation x4 -> x0, loops' own time: 16 us -> none  [the longest x2 8.1 us: attend(): mixed, log_total = lax.map(block_step, starts)]
    convert_element_type x9 -> x0, other arithmetic: 12.7 us -> none  [the longest x4 7.27 us: block_step(): grad_scores = (probs * (grad_probs - inner)).astype(jnp.bfloat16)]
  transfers between devices with their start and end apart: 20 -> 0, of which waited for: 18 -> 0; matrix products, arithmetic and copies ran while one was open for 17% -> 0% of each run, Pallas kernels for 0% -> 0%
where the time goes in v1:
time: 212 us; the launch traced here: 211 us
  Pallas kernels  190 us (90%)
  local copies, waits for them, and re-layouts  20.2 us (10%)
    pallas_call x1, Pallas kernels, body(): pl.pallas_call(functools.partial(block_kernel, n_dp, in_dp), out_shape=(j...  190 us
    reshape x7, local copies, waits for them, and re-layouts, body(): row = lambda v: v.reshape(1, -1)  8.87 us
    unnamed x13, local copies, waits for them, and re-layouts  8.05 us

profile of v1, /device:TPU:0, one launch (start us, length us, event | category | flops | bytes accessed | tf_op | source)
XLA Modules:
  0.0 211.2 jit_solution(15245749486912791915)
XLA Ops:
  0.6 1.3 reshape.84.gain1
  1.9 1.3 reshape.85.shift1
  3.2 1.3 reshape.87.bias_out
  4.4 1.3 reshape.88.gain2
  5.7 1.3 reshape.89.shift2
  7.0 1.3 reshape.90.bias_up
  8.2 1.3 reshape.91.bias_down
  9.5 1.3 copy_bitcast_fusion
  10.8 1.5 copy.34.bias_qv
  12.3 189.8 %vision_block.1 = (bf16[2,256,768]{2,1,0:T(8,128)(2,1)}, f32[2,256,768]{2,1,0:T(8,128)}, f32[8,768]{1,0:T(8,128)}, f32[1,576]{1,0:T(1,128)}, f32[96,1536]{1,0:T(8,128)}, /*index=5*/f32[96,768]{1,0:T(8,128)}) custom-call(bf16[2,256,768]{2,1,0:T(8,128)(2,1)} %bitcast.22, bf16[2,256,768]{2,1,0:T(8,128)(2,1)} %bitcast.23, s32[2,1024]{1,0:T(2,128)} %get-tuple-element.64.seg_ref, ...), custom_call_target="tpu_custom_call" | custom-call | tf_op jit(solution)/shard_map/vision_block/pallas_call | solution.py:734
  202.1 0.0 copy-start.3
  202.1 0.0 copy-start.2
  202.1 4.2 %copy.37 = f32[2,256,1,768]{3,2,1,0:T(1,128)} copy(f32[2,256,1,768]{3,1,0,2:T(8,128)} %bitcast.19) | data formatting | bytes 3145728
  206.4 0.0 copy-done.3
  206.4 0.0 copy-start.1
  206.4 0.6 pad_maximum_fusion
  207.0 0.7 slice_reduce_fusion
  207.6 0.0 copy-done.2
  207.6 0.0 copy-start
  207.6 0.1 slice_bitcast_fusion.1
  207.7 0.7 copy.39
  208.5 0.1 copy.35
  208.6 0.9 copy.38
  209.5 0.0 copy-done.1
  209.5 0.8 slice_bitcast_fusion
  210.4 0.0 copy-done
  210.4 0.9 copy.45
  (2 shorter events, 0.0 us)
Async XLA Ops:
  202.1 4.2 %copy-start.3 = (f32[8,768]{1,0:T(8,128)S(1)}, f32[8,768]{1,0:T(8,128)}, u32[]{:S(2)}) copy-start(f32[8,768]{1,0:T(8,128)} %get-tuple-element.21) | copy-start | bytes 73732
  202.1 5.5 %copy-start.2 = (f32[96,768]{1,0:T(8,128)S(1)}, f32[96,768]{1,0:T(8,128)}, u32[]{:S(2)}) copy-start(f32[96,768]{1,0:T(8,128)} %get-tuple-element.22) | copy-start | bytes 884740
  206.4 3.1 %copy-start.1 = (f32[96,1536]{1,0:T(8,128)S(1)}, f32[96,1536]{1,0:T(8,128)}, u32[]{:S(2)}) copy-start(f32[96,1536]{1,0:T(8,128)} %get-tuple-element.23) | copy-start | bytes 1769476
  207.6 2.7 %copy-start = (bf16[2,256,768]{2,1,0:T(8,128)(2,1)S(1)}, bf16[2,256,768]{2,1,0:T(8,128)(2,1)}, u32[]{:S(2)}) copy-start(bf16[2,256,768]{2,1,0:T(8,128)(2,1)} %get-tuple-element.19) | copy-start | bytes 2359300

commit v2 on v1

--- a/solution.py
+++ b/solution.py
@@ -90,9 +90,12 @@
     gtok_ref,
     small_ref,
     qvb_ref,
-    own_a,
-    own_b,
+    own_dn,
+    own_up,
+    own_o,
+    own_j,
     wq,
+    wkv,
     wo,
     wu,
     wd,
@@ -103,8 +106,7 @@
     qT,
     kT,
     vT,
-    kk,
-    vv,
+    kv,
     oT,
     lse,
     doT,
@@ -123,15 +125,18 @@
     ysend,
     yrecv,
     mid,
-    ga,
-    gb,
+    g_dn,
+    g_up,
+    g_o,
+    g_j,
     *rest,
 ):
     if in_dp:
-        xs_a, xr_a, zr_a, xs_b, xr_b, zr_b, vec, trecv, dsend, drecv, send_sem, recv_sem, w_sem = rest
+        stages, (vec, trecv, dsend, drecv, send_sem, recv_sem, w_sem) = rest[:12], rest[12:]
     else:
         vec, send_sem, recv_sem, w_sem = rest
     micro, R, D = x_ref.shape
+    line = lambda ref: ref[...].reshape(1, -1)
     L = 4 * R
     HL = wo.shape[0]
     FL = wu.shape[1]
@@ -160,6 +165,13 @@
         pltpu.make_async_copy(s, d, w_sem.at[i])
         for i, (s, d) in enumerate(((wqkv_hbm, wq), (wo_hbm, wo), (wu_hbm, wu), (wd_hbm, wd)))
     ]
+    for h in range(heads):
+        for j in range(2):
+            src = wqkv_hbm.at[pl.ds((1 + j) * HL + h * HEAD_DIM, HEAD_DIM), :]
+            dst = wkv.at[pl.ds((2 * h + j) * HEAD_DIM, HEAD_DIM), :]
+            loads.append(pltpu.make_async_copy(src, dst, w_sem.at[len(loads)]))
+    for m in range(micro):
+        loads.append(pltpu.make_async_copy(g_ref.at[m], g_all.at[m, 0], w_sem.at[len(loads)]))
     for ld in loads:
         ld.start()
 
@@ -251,34 +263,36 @@
     def first_norm(m):
         def step(rows):
             n, _ = norm_parts(x_ref[m, rows, :].astype(F32))
-            a_all[m, 0, rows, :] = (n * gain1[...] + shift1[...]).astype(BF16)
+            a_all[m, 0, rows, :] = (n * line(gain1) + line(shift1)).astype(BF16)
 
         by_rows(step)
 
     def codes(m):
         for r in range(4):
-            seg = seg_ref[pl.ds(m, 1), pl.ds(pl.multiple_of(blocks[r] * R, R), R)].astype(F32)
-            val = val_ref[pl.ds(m, 1), pl.ds(pl.multiple_of(blocks[r] * R, R), R)]
+            seg = seg_ref[m, :, pl.ds(pl.multiple_of(blocks[r] * R, R), R)].astype(F32)
+            val = val_ref[m, :, pl.ds(pl.multiple_of(blocks[r] * R, R), R)]
             place = lax.broadcasted_iota(jnp.int32, (1, R), 1).astype(F32) + (SELF_CODE + r * R)
             code = jnp.where(val > 0, seg, place)
             kcol[pl.ds(r * R, R), :] = jnp.broadcast_to(code, (128, R)).T
 
     def qkv(m):
+        cols_of = jnp.broadcast_to(bias_qv[...].reshape(2, 1, HL), (2, 8, HL))
+        bq = cols_of[0].T[:, :1]
+        bv = cols_of[1].T[:, :1]
+        none = jnp.zeros((1, HEAD_DIM), F32)
+        v_row = bias_qv[1:2, :]
+        kv_bias = jnp.concatenate([p for h in range(heads) for p in (none, v_row[:, h * HEAD_DIM : (h + 1) * HEAD_DIM])], axis=1)
+
         def slot(r):
             a = a_all[m, r]
             cols = slice(r * R, (r + 1) * R)
             allT = mm_nt(wq[...], a)
-            bq = bias_qv[0].reshape(HL, 1)
-            bv = bias_qv[1].reshape(HL, 1)
-            q_low = (allT[:HL] + bq).astype(BF16)
-            qT[m, :, cols] = q_low * jnp.asarray(scale, BF16)
+            qT[m, :, cols] = (allT[:HL] + bq).astype(BF16) * jnp.asarray(scale, BF16)
             kT[m, :, cols] = allT[HL : 2 * HL].astype(BF16)
             vT[m, :, cols] = (allT[2 * HL :] + bv).astype(BF16)
-            kv = mm_nt(a, wq[HL:, :])
+            both = mm_nt(a, wkv[...]) + kv_bias
             for h in range(heads):
-                kk[m, h, cols, :] = kv[:, h * HEAD_DIM : (h + 1) * HEAD_DIM].astype(BF16)
-                bv_row = jnp.broadcast_to(bv, (HL, 128)).T[:1, h * HEAD_DIM : (h + 1) * HEAD_DIM]
-                vv[m, h, cols, :] = (kv[:, HL + h * HEAD_DIM : HL + (h + 1) * HEAD_DIM] + bv_row).astype(BF16)
+                kv[m, h, cols, :] = both[:, h * 128 : (h + 1) * 128].astype(BF16)
 
         slot(0)
         ag_a[m].wait_core()
@@ -292,7 +306,7 @@
         cols = pl.ds(pl.multiple_of(qb * R, R), R)
         place = (lax.broadcasted_iota(jnp.int32, (1, R), 1) + qb * R).astype(F32) + SELF_CODE
         blk = jnp.where(qb == 0, blocks[0], jnp.where(qb == 1, blocks[1], jnp.where(qb == 2, blocks[2], blocks[3])))
-        seg = seg_ref[pl.ds(m, 1), pl.ds(pl.multiple_of(blk * R, R), R)].astype(F32)
+        seg = seg_ref[m, :, pl.ds(pl.multiple_of(blk * R, R), R)].astype(F32)
         for c in range(L // KC):
             kc = kcol[c * KC : (c + 1) * KC, :1]
             ok = (kc == seg) | (kc == place)
@@ -313,11 +327,11 @@
             @pl.loop(0, heads)
             def _(h):
                 hrows = pl.ds(pl.multiple_of(h * HEAD_DIM, HEAD_DIM), HEAD_DIM)
-                q = qT[m, hrows, cols]
+                q = jnp.concatenate([qT[m, hrows, cols], jnp.zeros((HEAD_DIM, R), BF16)], axis=0)
                 top8 = None
                 for c in range(L // KC):
                     rows = slice(c * KC, (c + 1) * KC)
-                    s = mm(kk[m, h, rows, :], q) + bias_scr[rows, :]
+                    s = mm(kv[m, h, rows, :], q) + bias_scr[rows, :]
                     s_scr[rows, :] = s
                     part8 = fold8(s, jnp.maximum)
                     top8 = part8 if top8 is None else jnp.maximum(top8, part8)
@@ -348,10 +362,10 @@
         rs_attn[m].arrive()
 
         def step(rows):
-            v = x_ref[m, rows, :].astype(F32) + (rs_attn[m].total(rows) + bias_out[...])
+            v = x_ref[m, rows, :].astype(F32) + (rs_attn[m].total(rows) + line(bias_out))
             mid[m, rows, :] = v
             n, _ = norm_parts(v)
-            c_all[m, 0, rows, :] = (n * gain2[...] + shift2[...]).astype(BF16)
+            c_all[m, 0, rows, :] = (n * line(gain2) + line(shift2)).astype(BF16)
 
         by_rows(step)
         ag_c[m].start_core()
@@ -362,7 +376,7 @@
         def _(r):
             rows = pl.ds(pl.multiple_of(r * R, R), R)
             g = g_all[m, r]
-            u = mm(c_all[m, r], wu[...]) + bias_up[...]
+            u = mm(c_all[m, r], wu[...]) + line(bias_up)
             dh = mm_nt(g, wd[...])
             th = jnp.tanh(GELU_A * (u + GELU_B * (u * u * u)))
             half_u = 0.5 * (1.0 + th)
@@ -385,11 +399,11 @@
                 down = mm_tn(g_all[m, r, :, f], h_scr[r * R : (r + 1) * R, :])
                 up = mm_tn(c_all[m, r, :, f], du_scr[r * R : (r + 1) * R, :])
                 if m == 0 and r == 0:
-                    ga[f, :FL] = down
-                    ga[f, FL:] = up
+                    g_dn[f, :] = down
+                    g_up[f, :] = up
                 else:
-                    ga[f, :FL] += down
-                    ga[f, FL:] += up
+                    g_dn[f, :] += down
+                    g_up[f, :] += up
 
     def add_row(i, v):
         vec[i : i + 1, :] += jnp.sum(v, axis=0, keepdims=True)
@@ -402,9 +416,9 @@
             n, r = norm_parts(mid[m, rows, :])
             add_row(3, dc * n)
             add_row(4, dc)
-            g = g_ref[m, rows, :].astype(F32)
+            g = g_all[m, 0, rows, :].astype(F32)
             add_row(5, g)
-            dx = g + norm_back(dc * gain2[...], n, r)
+            dx = g + norm_back(dc * line(gain2), n, r)
             gtok_ref[m, rows, :] = dx
             low = dx.astype(BF16)
             add_row(2, low.astype(F32))
@@ -414,7 +428,7 @@
         ag_d[m].start_core()
         ag_d[m].start_y()
 
-    def attend_back(m):
+    def attend_back(m, ready, hooks):
         def project(r):
             doT[:, r * R : (r + 1) * R] = mm_nt(wo[...], d_all[m, r]).astype(BF16)
 
@@ -425,6 +439,7 @@
         project(2)
         ag_d[m].wait_last()
         project(3)
+        ready()
         dkT[...] = jnp.zeros_like(dkT)
         dvT[...] = jnp.zeros_like(dvT)
 
@@ -439,16 +454,22 @@
                 do = doT[hrows, cols]
                 inner = jnp.sum(do.astype(F32) * oT[m, hrows, cols].astype(F32), axis=0, keepdims=True)
                 log_total = lse[m, pl.ds(h, 1), cols]
+                blank = jnp.zeros((HEAD_DIM, R), BF16)
+                q_rhs = jnp.concatenate([q, blank], axis=0)
+                do_rhs = jnp.concatenate([blank, do], axis=0)
                 for c in range(L // KC):
                     rows = slice(c * KC, (c + 1) * KC)
-                    s = mm(kk[m, h, rows, :], q) + bias_scr[rows, :]
+                    s = mm(kv[m, h, rows, :], q_rhs) + bias_scr[rows, :]
                     p = jnp.exp(s - log_total)
-                    dprob = mm(vv[m, h, rows, :], do)
+                    dprob = mm(kv[m, h, rows, :], do_rhs)
                     p_scr[rows, :] = p.astype(BF16)
                     ds_scr[rows, :] = (p * (dprob - inner)).astype(BF16)
                 dvT[hrows, :] += mm_nt(do, p_scr[...])
                 dkT[hrows, :] += mm_nt(q, ds_scr[...])
                 dqkvT[hrows, cols] = (mm(kT[m, hrows, :], ds_scr[...]) * scale).astype(BF16)
+
+            for at, hook in hooks.items():
+                pl.when(qb == at)(hook)
 
         dqkvT[HL : 2 * HL, :] = dkT[...].astype(BF16)
         dqkvT[2 * HL :, :] = dvT[...].astype(BF16)
@@ -461,6 +482,19 @@
                 rs.start_near()
                 rs.relay()
 
+    def out_sums(m):
+        B = min(256, D)
+
+        @pl.loop(0, D // B)
+        def _(i):
+            f = pl.ds(pl.multiple_of(i * B, B), B)
+            for r in range(4):
+                o = mm_tt(d_all[m, r, :, f], oT[m, :, r * R : (r + 1) * R])
+                if m == 0 and r == 0:
+                    g_o[f, :] = o
+                else:
+                    g_o[f, :] += o
+
     def head_sums(m):
         B = min(256, D)
         sums = mm_nt(jnp.ones((8, L), BF16), dqkvT[...])[:1]
@@ -473,21 +507,17 @@
         def _(i):
             f = pl.ds(pl.multiple_of(i * B, B), B)
             for r in range(4):
-                cols = slice(r * R, (r + 1) * R)
-                j = mm_tt(a_all[m, r, :, f], dqkvT[:, cols])
-                o = mm_tt(d_all[m, r, :, f], oT[m, :, cols])
+                j = mm_tt(a_all[m, r, :, f], dqkvT[:, r * R : (r + 1) * R])
                 if m == 0 and r == 0:
-                    gb[f, : 3 * HL] = j
-                    gb[f, 3 * HL :] = o
+                    g_j[f, :] = j
                 else:
-                    gb[f, : 3 * HL] += j
-                    gb[f, 3 * HL :] += o
+                    g_j[f, :] += j
 
     def finish_out(m):
         rs_branch[m].arrive()
 
         def step(rows):
-            out_ref[m, rows, :] = (mid[m, rows, :] + (rs_branch[m].total(rows) + bias_down[...])).astype(BF16)
+            out_ref[m, rows, :] = (mid[m, rows, :] + (rs_branch[m].total(rows) + line(bias_down))).astype(BF16)
 
         by_rows(step)
 
@@ -499,13 +529,13 @@
             n, r = norm_parts(x_ref[m, rows, :].astype(F32))
             add_row(0, da * n)
             add_row(1, da)
-            gtok_ref[m, rows, :] += norm_back(da * gain1[...], n, r)
+            gtok_ref[m, rows, :] += norm_back(da * line(gain1), n, r)
 
         by_rows(step)
 
     class Reduce:
-        def __init__(self, acc, xs, xr, zr, own):
-            self.acc, self.xs, self.xr, self.zr, self.own = acc, xs, xr, zr, own
+        def __init__(self, acc, xs, xr, zr):
+            self.acc, self.xs, self.xr, self.zr = acc, xs, xr, zr
             self.rows = D // n_dp
             self.n2 = n_dp // 2
             self.px = lax.rem(dp, 2)
@@ -538,21 +568,23 @@
             for off in range(1, self.n2):
                 self.z[off - 1].wait_recv()
                 tot = tot + self.zr[off - 1].astype(F32)
-            self.own[...] = tot
+            return tot
 
         def drain(self):
             for c in self.z:
                 c.wait_send()
 
     if in_dp:
-        red_a = Reduce(ga, xs_a, xr_a, zr_a, own_a)
-        red_b = Reduce(gb, xs_b, xr_b, zr_b, own_b)
+        dn, up, ro, rj = (Reduce(acc, *stages[3 * i : 3 * i + 3]) for i, acc in enumerate((g_dn, g_up, g_o, g_j)))
         small_t = [names.copy(vec, trecv.at[i], {"tensor": d}) for i, d in enumerate((t_core, t_y, t_diag))]
         small_d = [names.copy(dsend, drecv.at[off - 1], {"dp": lax.rem(dp + off, n_dp)}) for off in range(1, n_dp)]
 
+    def reduce(*steps):
+        if in_dp:
+            for step in steps:
+                step()
+
     vec[...] = jnp.zeros_like(vec)
-    for m in range(micro):
-        g_all[m, 0] = g_ref[m]
     first_norm(0)
     pl.semaphore_wait(barrier, met)
     ag_a[0].start_core()
@@ -561,12 +593,14 @@
         first_norm(m)
         ag_a[m].start_core()
         ag_a[m].start_y()
+    for ld in loads[4 + 2 * heads :]:
+        ld.wait()
     for m in range(micro):
         ag_g[m].start_core()
     ag_g[0].start_y()
     codes(0)
-    loads[0].wait()
-    loads[1].wait()
+    for ld in loads[:2] + loads[4 : 4 + 2 * heads]:
+        ld.wait()
 
     qkv(0)
     attend(0)
@@ -574,17 +608,17 @@
     codes(1)
     qkv(1)
     attend(1)
-    middle(0)
     attn_out(1)
-    ag_g[1].start_y()
     loads[2].wait()
     loads[3].wait()
 
-    def feed_all(m, between):
+    def feed_all(m, between, after):
         ag_c[m].wait_core()
         ag_g[m].wait_core()
         rs_attn[m].drain()
         feed(m, 0)
+        rs_dc[m].start_near()
+        rs_branch[m].start_near()
         between()
         ag_c[m].forward()
         ag_g[m].forward()
@@ -592,37 +626,57 @@
         ag_g[m].wait_last()
         feed(m, 2)
         rs_dc[m].start_far()
-        rs_dc[m].start_near()
         rs_dc[m].relay()
         rs_branch[m].start_far()
-        rs_branch[m].start_near()
-        rs_branch[m].relay()
+        after()
         weight_sums(m)
 
-    feed_all(0, lambda: middle(1))
-    feed_all(1, lambda: turn(0))
-    if in_dp:
-        red_a.start()
-    turn(1)
+    middle(0)
+    feed_all(0, lambda: middle(1), lambda: ag_g[1].start_y())
+    feed_all(1, lambda: turn(0), lambda: None)
+    if in_dp:
+        reduce(dn.start, up.start)
+
+    def late_turn():
+        turn(1)
+        if in_dp:
+            reduce(dn.second)
+
     codes(0)
     rs_dc[0].drain()
-    attend_back(0)
+    attend_back(0, lambda: out_sums(0), {2: late_turn})
+    rs_branch[0].relay()
     head_sums(0)
-    finish_out(0)
-    finish_out(1)
-    if in_dp:
-        red_a.second()
     codes(1)
     rs_dc[1].drain()
-    attend_back(1)
+
+    def out_ready():
+        out_sums(1)
+        if in_dp:
+            reduce(ro.start)
+
+    def mid_back():
+        if in_dp:
+            reduce(up.second)
+
+    def late_back():
+        if in_dp:
+            reduce(ro.second)
+
+    attend_back(1, out_ready, {0: mid_back, 2: late_back})
+    rs_branch[1].relay()
     head_sums(1)
     if in_dp:
-        red_b.start()
-        red_a.last()
+        rj.start()
     finish_in(0)
+    finish_out(0)
+    if in_dp:
+        own_dn[...] = dn.last()
+        own_up[...] = up.last()
+        own_o[...] = ro.last()
+        rj.second()
     finish_in(1)
     if in_dp:
-        red_b.second()
         vec[7:8, : 3 * HL] = qvb_ref[...]
         for c in small_t:
             c.start()
@@ -632,7 +686,11 @@
         dsend[...] = vec[...] + jnp.where(six, trecv[0] + trecv[1] + trecv[2], 0.0)
         for c in small_d:
             c.start()
-        red_b.last()
+    finish_out(1)
+    if in_dp:
+        tot = rj.last()
+        for i in range(3):
+            own_j[i] = tot[:, i * HL : (i + 1) * HL]
         tot = dsend[...]
         for i, c in enumerate(small_d):
             c.wait_recv()
@@ -640,12 +698,15 @@
         small_ref[...] = tot
         for c in small_t + small_d:
             c.wait_send()
-        red_a.drain()
-        red_b.drain()
+        for r in (dn, up, ro, rj):
+            r.drain()
     else:
         small_ref[...] = vec[...]
-        own_a[...] = ga[...]
-        own_b[...] = gb[...]
+        own_dn[...] = g_dn[...]
+        own_up[...] = g_up[...]
+        own_o[...] = g_o[...]
+        for i in range(3):
+            own_j[i] = g_j[:, i * HL : (i + 1) * HL]
     for m in range(micro):
         rs_branch[m].drain()
         rs_da[m].drain()
@@ -679,14 +740,14 @@
     heads = HL // HEAD_DIM
     in_dp = n_dp > 1 and n_dp % 2 == 0 and D % n_dp == 0 and (D // n_dp) % 16 == 0
     n2, rows = n_dp // 2, D // n_dp
-    row = lambda v: v.reshape(1, -1)
     wqT = jnp.transpose(w_qkv, (1, 2, 0)).reshape(3 * HL, D)
     vmem = pl.BlockSpec(memory_space=pltpu.VMEM)
     hbm = pl.BlockSpec(memory_space=pl.ANY)
     own_rows = rows if in_dp else D
-    ca, cb = 2 * FL, 4 * HL
+    widths = (FL, FL, HL, 3 * HL)
     scratch = [
         pltpu.VMEM((3 * HL, D), BF16),
+        pltpu.VMEM((2 * HL, D), BF16),
         pltpu.VMEM((HL, D), BF16),
         pltpu.VMEM((D, FL), BF16),
         pltpu.VMEM((FL, D), BF16),
@@ -697,8 +758,7 @@
         pltpu.VMEM((micro, HL, L), BF16),
         pltpu.VMEM((micro, HL, L), BF16),
         pltpu.VMEM((micro, HL, L), BF16),
-        pltpu.VMEM((micro, heads, L, HEAD_DIM), BF16),
-        pltpu.VMEM((micro, heads, L, HEAD_DIM), BF16),
+        pltpu.VMEM((micro, heads, L, 2 * HEAD_DIM), BF16),
         pltpu.VMEM((micro, HL, L), BF16),
         pltpu.VMEM((micro, heads, L), F32),
         pltpu.VMEM((HL, L), BF16),
@@ -717,11 +777,10 @@
         pltpu.VMEM((2 * micro, R, D), BF16),
         pltpu.VMEM((2 * micro, R, D), BF16),
         pltpu.VMEM((micro, R, D), F32),
-        pltpu.VMEM((D, ca), F32),
-        pltpu.VMEM((D, cb), F32),
+        *(pltpu.VMEM((D, c), F32) for c in widths),
     ]
     if in_dp:
-        for c in (ca, cb):
+        for c in widths:
             scratch += [
                 pltpu.VMEM((n2, rows, c), BF16),
                 pltpu.VMEM((n2, rows, c), BF16),
@@ -730,7 +789,7 @@
     scratch += [pltpu.VMEM((8, D), F32)]
     if in_dp:
         scratch += [pltpu.VMEM((3, 8, D), F32), pltpu.VMEM((8, D), F32), pltpu.VMEM((n_dp - 1, 8, D), F32)]
-    scratch += [pltpu.SemaphoreType.DMA((SEMS,)), pltpu.SemaphoreType.DMA((SEMS,)), pltpu.SemaphoreType.DMA((4,))]
+    scratch += [pltpu.SemaphoreType.DMA((SEMS,)), pltpu.SemaphoreType.DMA((SEMS,)), pltpu.SemaphoreType.DMA((6 + 2 * heads,))]
     outs = pl.pallas_call(
         functools.partial(block_kernel, n_dp, in_dp),
         out_shape=(
@@ -738,11 +797,13 @@
             jax.ShapeDtypeStruct((micro, R, D), F32),
             jax.ShapeDtypeStruct((8, D), F32),
             jax.ShapeDtypeStruct((1, 3 * HL), F32),
-            jax.ShapeDtypeStruct((own_rows, ca), F32),
-            jax.ShapeDtypeStruct((own_rows, cb), F32),
+            jax.ShapeDtypeStruct((own_rows, FL), F32),
+            jax.ShapeDtypeStruct((own_rows, FL), F32),
+            jax.ShapeDtypeStruct((own_rows, HL), F32),
+            jax.ShapeDtypeStruct((3, own_rows, HL), F32),
         ),
-        in_specs=[vmem] * 12 + [hbm] * 4,
-        out_specs=[vmem] * 6,
+        in_specs=[vmem, hbm] + [vmem] * 10 + [hbm] * 4,
+        out_specs=[vmem] * 8,
         scratch_shapes=scratch,
         compiler_params=pltpu.CompilerParams(
             collective_id=0, has_side_effects=True, vmem_limit_bytes=67043328
@@ -751,45 +812,44 @@
     )(
         tokens.reshape(micro, R, D),
         out_grad.reshape(micro, R, D),
-        segment_ids.reshape(micro, L),
-        valid_mask.reshape(micro, L),
-        row(gain_one),
-        row(shift_one),
-        bias_qv.reshape(2, HL, 1),
-        row(bias_out),
-        row(gain_two),
-        row(shift_two),
-        row(bias_up),
-        row(bias_down),
+        segment_ids,
+        valid_mask,
+        gain_one,
+        shift_one,
+        bias_qv,
+        bias_out,
+        gain_two,
+        shift_two,
+        bias_up,
+        bias_down,
         wqT,
         output_weight,
         up_weight,
         down_weight,
     )
-    out, gtok, small, qvb, share_a, share_b = outs
+    out, gtok, small, qvb, share_dn, share_up, share_o, share_j = outs
     if not in_dp:
-        share_a, share_b = (lax.psum_scatter(v, "dp", scatter_dimension=0, tiled=True) for v in (share_a, share_b))
+        share_dn, share_up, share_o = (lax.psum_scatter(v, "dp", scatter_dimension=0, tiled=True) for v in (share_dn, share_up, share_o))
+        share_j = lax.psum_scatter(share_j, "dp", scatter_dimension=1, tiled=True)
         small = jnp.concatenate([lax.psum(small[:6], ("dp", "tensor")), lax.psum(small[6:7], "dp")])
         sums = lax.psum(qvb[0], "dp")
     else:
         sums = small[7, : 3 * HL]
-    own_rows = share_a.shape[0]
-    grad_qkv = share_b[:, : 3 * HL].reshape(own_rows, 3, HL)
     grad_bias_qv = jnp.stack([sums[:HL], sums[2 * HL :]])
     return (
         out.reshape(micro, R, 1, D),
         gtok.reshape(micro, R, 1, D),
         small[0],
         small[1],
-        grad_qkv,
+        jnp.transpose(share_j, (1, 0, 2)),
         grad_bias_qv,
-        share_b[:, 3 * HL :].T,
+        share_o.T,
         small[2],
         small[3],
         small[4],
-        share_a[:, FL:],
+        share_up,
         small[6, :FL],
-        share_a[:, :FL].T,
+        share_dn.T,
         small[5],
     )
 

time: 212 us -> 185 us (0.87)
  Pallas kernels: 190 us -> 175 us
  local copies, waits for them, and re-layouts: 20.2 us -> 8.69 us
    pallas_call x1, Pallas kernels: 190 us -> 175 us  [body(): pl.pallas_call(functools.partial(block_kernel, n_dp, in_dp), out_shape=(j...]
    reshape x8 -> x0, local copies, waits for them, and re-layouts: 10.4 us -> none  [the longest x7 8.87 us: body(): row = lambda v: v.reshape(1, -1)]
    unnamed x13 -> x18, local copies, waits for them, and re-layouts: 8.05 us -> 8.03 us
where the time goes in v2:
time: 185 us
  Pallas kernels  175 us (95%)
  local copies, waits for them, and re-layouts  8.69 us (5%)
    pallas_call x1, Pallas kernels, body(): pl.pallas_call(functools.partial(block_kernel, n_dp, in_dp), out_shape=(j...  175 us
    unnamed x18, local copies, waits for them, and re-layouts  8.03 us

profile of v2, /device:TPU:0, one launch (start us, length us, event | category | flops | bytes accessed | tf_op | source)
XLA Modules:
  0.0 184.9 jit_solution(15771609925863990577)
XLA Ops:
  0.7 175.0 %vision_block.1 = (bf16[2,256,768]{2,1,0:T(8,128)(2,1)}, f32[2,256,768]{2,1,0:T(8,128)}, f32[8,768]{1,0:T(8,128)}, f32[1,576]{1,0:T(1,128)}, f32[96,768]{1,0:T(8...) custom-call(bf16[2,256,768]{2,1,0:T(8,128)(2,1)} %bitcast.15, bf16[2,256,768]{2,1,0:T(8,128)(2,1)} %bitcast.16, ...), custom_call_target="tpu_custom_call" | custom-call | tf_op jit(solution)/shard_map/vision_block/pallas_call | solution.py:793
  175.6 0.0 copy-start.5
  175.6 0.0 copy-start.4
  175.6 0.0 copy-start
  175.7 4.2 %copy.31 = f32[2,256,1,768]{3,2,1,0:T(1,128)} copy(f32[2,256,1,768]{3,1,0,2:T(8,128)} %bitcast.12) | data formatting | bytes 3145728
  179.9 0.0 copy-done.5
  179.9 0.0 copy-start.3
  179.9 0.0 copy-start.2
  179.9 0.0 copy-start.1
  179.9 0.6 pad_maximum_fusion
  180.5 0.7 slice_reduce_fusion
  181.2 0.0 copy-done.4
  181.2 0.7 copy.32
  181.9 0.0 copy-done
  181.9 0.9 copy.37
  182.8 0.0 copy-done.3
  182.8 0.7 copy.38
  183.5 0.0 copy-done.2
  183.5 0.7 copy.39
  184.2 0.0 copy-done.1
  184.2 0.7 copy.40
  (1 shorter events, 0.0 us)
Async XLA Ops:
  175.6 4.3 %copy-start.5 = (f32[8,768]{1,0:T(8,128)S(1)}, f32[8,768]{1,0:T(8,128)}, u32[]{:S(2)}) copy-start(f32[8,768]{1,0:T(8,128)} %get-tuple-element.23) | copy-start | bytes 73732
  175.6 5.5 %copy-start.4 = (f32[96,192]{1,0:T(8,128)S(1)}, f32[96,192]{1,0:T(8,128)}, u32[]{:S(2)}) copy-start(f32[96,192]{1,0:T(8,128)} %get-tuple-element.25) | copy-start | bytes 221188
  175.6 6.3 %copy-start = (bf16[2,256,768]{2,1,0:T(8,128)(2,1)S(1)}, bf16[2,256,768]{2,1,0:T(8,128)(2,1)}, u32[]{:S(2)}) copy-start(bf16[2,256,768]{2,1,0:T(8,128)(2,1)} %get-tuple-element.21) | copy-start | bytes 2359300
  179.9 2.9 %copy-start.3 = (f32[3,96,192]{2,1,0:T(8,128)S(1)}, f32[3,96,192]{2,1,0:T(8,128)}, u32[]{:S(2)}) copy-start(f32[3,96,192]{2,1,0:T(8,128)} %get-tuple-element.24) | copy-start | bytes 663556
  179.9 3.6 %copy-start.2 = (f32[96,768]{1,0:T(8,128)S(1)}, f32[96,768]{1,0:T(8,128)}, u32[]{:S(2)}) copy-start(f32[96,768]{1,0:T(8,128)} %get-tuple-element.75) | copy-start | bytes 884740
  179.9 4.3 %copy-start.1 = (f32[96,768]{1,0:T(8,128)S(1)}, f32[96,768]{1,0:T(8,128)}, u32[]{:S(2)}) copy-start(f32[96,768]{1,0:T(8,128)} %get-tuple-element.27) | copy-start | bytes 884740

commit v3 on v2

--- a/solution.py
+++ b/solution.py
@@ -128,11 +128,12 @@
     g_dn,
     g_up,
     g_o,
-    g_j,
+    g_q,
+    g_kv,
     *rest,
 ):
     if in_dp:
-        stages, (vec, trecv, dsend, drecv, send_sem, recv_sem, w_sem) = rest[:12], rest[12:]
+        stages, (vec, trecv, dsend, drecv, send_sem, recv_sem, w_sem) = rest[:15], rest[15:]
     else:
         vec, send_sem, recv_sem, w_sem = rest
     micro, R, D = x_ref.shape
@@ -175,7 +176,7 @@
     for ld in loads:
         ld.start()
 
-    CH = min(64, R)
+    CH = min(64, R // 2)
     KC = min(128, R)
 
     half = R // 2
@@ -190,9 +191,9 @@
         def start_core(self):
             self.core.start()
 
-        def start_y(self):
-            for c in self.y:
-                c.start()
+        def start_y(self, *which):
+            for i in which or (0, 1):
+                self.y[i].start()
 
         def wait_core(self):
             self.core.wait_recv()
@@ -215,7 +216,8 @@
             self.p = p
             self.c3 = names.copy(part.at[p, 3], crecv.at[p, 1], core)
             self.c1 = names.copy(part.at[p, 1], crecv.at[p, 0], core)
-            self.y = names.copy(ysend.at[p], yrecv.at[p], ydev)
+            self.y = [names.copy(ysend.at[p, pl.ds(i * half, half)], yrecv.at[p, pl.ds(i * half, half)], ydev) for i in range(2)]
+            self.met = False
 
         def start_far(self):
             self.c3.start()
@@ -223,27 +225,31 @@
         def start_near(self):
             self.c1.start()
 
-        def relay(self):
+        def relay(self, *which):
             p = self.p
-            self.c3.wait_recv()
-
-            @pl.loop(0, R // CH)
-            def _(i):
-                rows = pl.ds(pl.multiple_of(i * CH, CH), CH)
-                ysend[p, rows, :] = (part[p, 2, rows, :].astype(F32) + crecv[p, 1, rows, :].astype(F32)).astype(BF16)
-
-            self.y.start()
+            if not self.met:
+                self.c3.wait_recv()
+                self.met = True
+            for i in which or (0, 1):
+
+                @pl.loop(i * half // CH, (i + 1) * half // CH)
+                def _(n):
+                    rows = pl.ds(pl.multiple_of(n * CH, CH), CH)
+                    ysend[p, rows, :] = (part[p, 2, rows, :].astype(F32) + crecv[p, 1, rows, :].astype(F32)).astype(BF16)
+
+                self.y[i].start()
 
         def arrive(self):
             self.c1.wait_recv()
-            self.y.wait_recv()
+            for c in self.y:
+                c.wait_recv()
 
         def total(self, rows):
             p = self.p
             return part[p, 0, rows, :].astype(F32) + crecv[p, 0, rows, :].astype(F32) + yrecv[p, rows, :].astype(F32)
 
         def drain(self):
-            for c in (self.c3, self.c1, self.y):
+            for c in [self.c3, self.c1] + self.y:
                 c.wait_send()
 
     def by_rows(step):
@@ -356,7 +362,7 @@
                 rs.start_far()
             if r == 1:
                 rs.start_near()
-                rs.relay()
+        rs.relay()
 
     def middle(m):
         rs_attn[m].arrive()
@@ -371,10 +377,11 @@
         ag_c[m].start_core()
         ag_c[m].start_y()
 
-    def feed(m, first):
+    def feed(m, first, last_slot):
         @pl.loop(first, first + 2)
         def _(r):
             rows = pl.ds(pl.multiple_of(r * R, R), R)
+            pl.when(r == 3)(last_slot)
             g = g_all[m, r]
             u = mm(c_all[m, r], wu[...]) + line(bias_up)
             dh = mm_nt(g, wd[...])
@@ -480,7 +487,7 @@
                 rs.start_far()
             if r == 1:
                 rs.start_near()
-                rs.relay()
+        rs.relay()
 
     def out_sums(m):
         B = min(256, D)
@@ -495,7 +502,7 @@
                 else:
                     g_o[f, :] += o
 
-    def head_sums(m):
+    def head_sums(m, kv_done, q_done):
         B = min(256, D)
         sums = mm_nt(jnp.ones((8, L), BF16), dqkvT[...])[:1]
         if m == 0:
@@ -503,15 +510,19 @@
         else:
             qvb_ref[...] += sums
 
-        @pl.loop(0, D // B)
-        def _(i):
-            f = pl.ds(pl.multiple_of(i * B, B), B)
-            for r in range(4):
-                j = mm_tt(a_all[m, r, :, f], dqkvT[:, r * R : (r + 1) * R])
-                if m == 0 and r == 0:
-                    g_j[f, :] = j
-                else:
-                    g_j[f, :] += j
+        for acc, lo, hi, done in ((g_kv, HL, 3 * HL, kv_done), (g_q, 0, HL, q_done)):
+
+            @pl.loop(0, D // B)
+            def _(i):
+                f = pl.ds(pl.multiple_of(i * B, B), B)
+                for r in range(4):
+                    j = mm_tt(a_all[m, r, :, f], dqkvT[lo:hi, r * R : (r + 1) * R])
+                    if m == 0 and r == 0:
+                        acc[f, :] = j
+                    else:
+                        acc[f, :] += j
+
+            done()
 
     def finish_out(m):
         rs_branch[m].arrive()
@@ -575,7 +586,7 @@
                 c.wait_send()
 
     if in_dp:
-        dn, up, ro, rj = (Reduce(acc, *stages[3 * i : 3 * i + 3]) for i, acc in enumerate((g_dn, g_up, g_o, g_j)))
+        dn, up, ro, rq, rkv = (Reduce(acc, *stages[3 * i : 3 * i + 3]) for i, acc in enumerate((g_dn, g_up, g_o, g_q, g_kv)))
         small_t = [names.copy(vec, trecv.at[i], {"tensor": d}) for i, d in enumerate((t_core, t_y, t_diag))]
         small_d = [names.copy(dsend, drecv.at[off - 1], {"dp": lax.rem(dp + off, n_dp)}) for off in range(1, n_dp)]
 
@@ -598,6 +609,7 @@
     for m in range(micro):
         ag_g[m].start_core()
     ag_g[0].start_y()
+    ag_g[1].start_y(0)
     codes(0)
     for ld in loads[:2] + loads[4 : 4 + 2 * heads]:
         ld.wait()
@@ -605,6 +617,7 @@
     qkv(0)
     attend(0)
     attn_out(0)
+    ag_g[1].start_y(1)
     codes(1)
     qkv(1)
     attend(1)
@@ -616,15 +629,18 @@
         ag_c[m].wait_core()
         ag_g[m].wait_core()
         rs_attn[m].drain()
-        feed(m, 0)
+        feed(m, 0, lambda: None)
         rs_dc[m].start_near()
         rs_branch[m].start_near()
         between()
         ag_c[m].forward()
         ag_g[m].forward()
-        ag_c[m].wait_last()
-        ag_g[m].wait_last()
-        feed(m, 2)
+
+        def last_slot():
+            ag_c[m].wait_last()
+            ag_g[m].wait_last()
+
+        feed(m, 2, last_slot)
         rs_dc[m].start_far()
         rs_dc[m].relay()
         rs_branch[m].start_far()
@@ -632,8 +648,8 @@
         weight_sums(m)
 
     middle(0)
-    feed_all(0, lambda: middle(1), lambda: ag_g[1].start_y())
-    feed_all(1, lambda: turn(0), lambda: None)
+    feed_all(0, lambda: middle(1), lambda: None)
+    feed_all(1, lambda: turn(0), lambda: rs_branch[0].relay(0))
     if in_dp:
         reduce(dn.start, up.start)
 
@@ -645,8 +661,9 @@
     codes(0)
     rs_dc[0].drain()
     attend_back(0, lambda: out_sums(0), {2: late_turn})
-    rs_branch[0].relay()
-    head_sums(0)
+    rs_branch[0].relay(1)
+    rs_branch[1].relay(0)
+    head_sums(0, lambda: None, lambda: None)
     codes(1)
     rs_dc[1].drain()
 
@@ -664,22 +681,25 @@
             reduce(ro.second)
 
     attend_back(1, out_ready, {0: mid_back, 2: late_back})
-    rs_branch[1].relay()
-    head_sums(1)
-    if in_dp:
-        rj.start()
+    if in_dp:
+        head_sums(1, rkv.start, rq.start)
+    else:
+        head_sums(1, lambda: None, lambda: None)
     finish_in(0)
     finish_out(0)
     if in_dp:
         own_dn[...] = dn.last()
         own_up[...] = up.last()
         own_o[...] = ro.last()
-        rj.second()
+        rkv.second()
+        rq.second()
     finish_in(1)
     if in_dp:
         vec[7:8, : 3 * HL] = qvb_ref[...]
         for c in small_t:
             c.start()
+    rs_branch[1].relay(1)
+    if in_dp:
         for c in small_t:
             c.wait_recv()
         six = lax.broadcasted_iota(jnp.int32, vec.shape, 0) < 6
@@ -688,9 +708,10 @@
             c.start()
     finish_out(1)
     if in_dp:
-        tot = rj.last()
-        for i in range(3):
-            own_j[i] = tot[:, i * HL : (i + 1) * HL]
+        tot = rkv.last()
+        own_j[1] = tot[:, :HL]
+        own_j[2] = tot[:, HL:]
+        own_j[0] = rq.last()
         tot = dsend[...]
         for i, c in enumerate(small_d):
             c.wait_recv()
@@ -698,15 +719,16 @@
         small_ref[...] = tot
         for c in small_t + small_d:
             c.wait_send()
-        for r in (dn, up, ro, rj):
+        for r in (dn, up, ro, rq, rkv):
             r.drain()
     else:
         small_ref[...] = vec[...]
         own_dn[...] = g_dn[...]
         own_up[...] = g_up[...]
         own_o[...] = g_o[...]
-        for i in range(3):
-            own_j[i] = g_j[:, i * HL : (i + 1) * HL]
+        own_j[0] = g_q[...]
+        own_j[1] = g_kv[:, :HL]
+        own_j[2] = g_kv[:, HL:]
     for m in range(micro):
         rs_branch[m].drain()
         rs_da[m].drain()
@@ -744,7 +766,7 @@
     vmem = pl.BlockSpec(memory_space=pltpu.VMEM)
     hbm = pl.BlockSpec(memory_space=pl.ANY)
     own_rows = rows if in_dp else D
-    widths = (FL, FL, HL, 3 * HL)
+    widths = (FL, FL, HL, HL, 2 * HL)
     scratch = [
         pltpu.VMEM((3 * HL, D), BF16),
         pltpu.VMEM((2 * HL, D), BF16),

time: 185 us -> 174 us (0.941)
  Pallas kernels: 175 us -> 164 us
    pallas_call x1, Pallas kernels: 175 us -> 164 us  [body(): pl.pallas_call(functools.partial(block_kernel, n_dp, in_dp), out_shape=(j...]
where the time goes in v3:
time: 174 us
  Pallas kernels  164 us (94%)
  local copies, waits for them, and re-layouts  8.69 us (5%)
    pallas_call x1, Pallas kernels, body(): pl.pallas_call(functools.partial(block_kernel, n_dp, in_dp), out_shape=(j...  164 us
    unnamed x18, local copies, waits for them, and re-layouts  8.03 us

profile of v3, /device:TPU:0, one launch (start us, length us, event | category | flops | bytes accessed | tf_op | source)
XLA Modules:
  0.0 174.3 jit_solution(14973384883058925933)
XLA Ops:
  0.7 164.3 %vision_block.1 = (bf16[2,256,768]{2,1,0:T(8,128)(2,1)}, f32[2,256,768]{2,1,0:T(8,128)}, f32[8,768]{1,0:T(8,128)}, f32[1,576]{1,0:T(1,128)}, f32[96,768]{1,0:T(8...) custom-call(bf16[2,256,768]{2,1,0:T(8,128)(2,1)} %bitcast.15, bf16[2,256,768]{2,1,0:T(8,128)(2,1)} %bitcast.16, ...), custom_call_target="tpu_custom_call" | custom-call | tf_op jit(solution)/shard_map/vision_block/pallas_call | solution.py:815
  165.0 0.0 copy-start.5
  165.0 0.0 copy-start.4
  165.0 0.0 copy-start
  165.0 4.2 %copy.31 = f32[2,256,1,768]{3,2,1,0:T(1,128)} copy(f32[2,256,1,768]{3,1,0,2:T(8,128)} %bitcast.12) | data formatting | bytes 3145728
  169.2 0.0 copy-done.5
  169.2 0.0 copy-start.3
  169.2 0.0 copy-start.2
  169.2 0.0 copy-start.1
  169.3 0.6 pad_maximum_fusion
  169.9 0.7 slice_reduce_fusion
  170.5 0.0 copy-done.4
  170.5 0.7 copy.32
  171.2 0.0 copy-done
  171.3 0.9 copy.37
  172.1 0.0 copy-done.3
  172.1 0.7 copy.38
  172.8 0.0 copy-done.2
  172.9 0.7 copy.39
  173.6 0.0 copy-done.1
  173.6 0.7 copy.40
  (1 shorter events, 0.0 us)
Async XLA Ops:
  165.0 4.3 %copy-start.5 = (f32[8,768]{1,0:T(8,128)S(1)}, f32[8,768]{1,0:T(8,128)}, u32[]{:S(2)}) copy-start(f32[8,768]{1,0:T(8,128)} %get-tuple-element.23) | copy-start | bytes 73732
  165.0 5.5 %copy-start.4 = (f32[96,192]{1,0:T(8,128)S(1)}, f32[96,192]{1,0:T(8,128)}, u32[]{:S(2)}) copy-start(f32[96,192]{1,0:T(8,128)} %get-tuple-element.25) | copy-start | bytes 221188
  165.0 6.3 %copy-start = (bf16[2,256,768]{2,1,0:T(8,128)(2,1)S(1)}, bf16[2,256,768]{2,1,0:T(8,128)(2,1)}, u32[]{:S(2)}) copy-start(bf16[2,256,768]{2,1,0:T(8,128)(2,1)} %get-tuple-element.21) | copy-start | bytes 2359300
  169.2 2.9 %copy-start.3 = (f32[3,96,192]{2,1,0:T(8,128)S(1)}, f32[3,96,192]{2,1,0:T(8,128)}, u32[]{:S(2)}) copy-start(f32[3,96,192]{2,1,0:T(8,128)} %get-tuple-element.24) | copy-start | bytes 663556
  169.2 3.6 %copy-start.2 = (f32[96,768]{1,0:T(8,128)S(1)}, f32[96,768]{1,0:T(8,128)}, u32[]{:S(2)}) copy-start(f32[96,768]{1,0:T(8,128)} %get-tuple-element.75) | copy-start | bytes 884740
  169.2 4.3 %copy-start.1 = (f32[96,768]{1,0:T(8,128)S(1)}, f32[96,768]{1,0:T(8,128)}, u32[]{:S(2)}) copy-start(f32[96,768]{1,0:T(8,128)} %get-tuple-element.27) | copy-start | bytes 884740
